TPU v7x, 256 devices: a whole 4x4x8 slice. The times are simulated.
256 devices in a mesh: hel: 8 (over y_hi, x), grid: 32 (over z, y_lo, core).
Axes of the slice: x: 4, y: 4 (y_hi: 2, y_lo: 2; y = y_hi * 2 + y_lo), z: 8, core: 2. Of those that a mesh axis runs over, the one named last changes fastest.
Arguments:
- phi_prev: float32 [16, 1536, 4096], P('hel', 'grid'), may hold values from -6 to 6
- phi_curr: float32 [16, 1536, 4096], P('hel', 'grid'), may hold values from -6 to 6
- helicity: int32 [16], replicated, may hold values from 0 to 18, as said below
- band: int32 [1536], P('grid'), may hold values from 0 to 47
- rotation: float32 [1536], P('grid'), may hold values from 0.2 to 0.8
- coupling: float32 [1536], P('grid'), may hold values from 0.3 to 1
- damping: float32 [4096], replicated, may hold values from 0.6 to 1
- potential: float32 [1536, 4096], P(None, 'grid'), may hold values from -0.6 to 0.6
- transform: bfloat16 [1536, 1536], P('grid'), may hold values from -0.15625 to 0.15625
- radial_long: float32 [128, 128], replicated, may hold values from -0.5 to 0.5
- radial_short: float32 [32, 32], replicated, may hold values from -1 to 1
Outputs:
- phi_next: float32 [16, 1536, 4096], P('hel', 'grid')
- phi_after: float32 [16, 1536, 4096], P('hel', 'grid')
Inputs may be any that keep to these rules, and one draw needn't show every extreme that they name: `helicity`: starts at 0 and is strictly increasing over the blocks; neighbouring blocks differ by 1 or 2, by 2 at exactly 3 places.
All inputs are finite; a program needn't handle non-finite values.
Results may differ from a plain program's by a relative error of at most 0.0013.
Values may be sent and summed in bfloat16 or wider, within the bound.
No kernel may reach another device: no remote copies, remote signals or barrier semaphores. Data moves between devices by JAX's collectives and lax.ppermute only.
A program may use at most 128 MiB of HBM per device.

v0:
```python
import functools
import jax
import jax.numpy as jnp
from jax import lax
from jax.experimental import pallas as pl
from jax.experimental.pallas import tpu as pltpu
from jax.sharding import Mesh, PartitionSpec as P

JMAX = 48
HEL = ("y_hi", "x")
GRID = ("z", "y_lo", "core")
VMEM = pl.BlockSpec(memory_space=pltpu.VMEM)
SMEM = pl.BlockSpec(memory_space=pltpu.SMEM)
PARAMS = pltpu.CompilerParams(vmem_limit_bytes=48 << 20)
F32, BF16, F16 = jnp.float32, jnp.bfloat16, jnp.float16


def split(x):
    high = x.astype(BF16)
    return high, (x - high.astype(F32)).astype(BF16)


def dot(a, b):
    return jnp.dot(a, b, preferred_element_type=F32)


def pack(v, dtype):
    return v.astype(dtype).reshape(2, 48, 32, 128).transpose(2, 0, 1, 3).reshape(32, 96, 128)


def local_kernel(prev_ref, coef_ref, damp_ref, long_ref, short_ref, *refs):
    if len(refs) == 4:
        (v_ref, out_ref, z_ref, y_ref), pot_ref = refs, None
    else:
        base_ref, pot_ref, v_ref, out_ref, z_ref, y_ref = refs

    def load(k, j):
        at = pl.ds(pl.multiple_of(j * 128, 128), 128)
        if pot_ref is None:
            return v_ref[k, :, at]
        pot = pot_ref[j, 48 * k : 48 * k + 48, :].astype(F32)
        v = base_ref[k, :, at] + 2.0 * damp_ref[:, at] * pot
        v_ref[k, :, at] = v
        return v

    def halves(ref):
        high, low = split(0.5 * (ref[...] + ref[...].T))
        top = jnp.concatenate([high, high], axis=1)
        return jnp.concatenate([top, jnp.concatenate([low, jnp.zeros_like(low)], axis=1)], axis=0)

    long_kin, short_kin = halves(long_ref), halves(short_ref)
    pad = jnp.zeros((32, 128), F32)

    def times(kin, one, two):
        high, low = split(jnp.concatenate([one, two], axis=1))
        both = dot(kin, jnp.concatenate([high, low], axis=0))
        return both[0:128] + both[128:256]

    def first(i, _):
        z = []
        for n in range(2):
            at = pl.ds(pl.multiple_of(i * 256 + n * 128, 128), 128)
            z.append(jnp.concatenate([load(0, 2 * i + n), load(1, 2 * i + n), pad], axis=0).T)
            z_ref[at, :] = z[n]
        y = times(short_kin, *z)
        for n in range(2):
            at = pl.ds(pl.multiple_of(i * 256 + n * 128, 128), 128)
            y_ref[at, :] = y[:, 128 * n : 128 * n + 128]
        return 0

    lax.fori_loop(0, 16, first, 0, unroll=4)

    def second(m, _):
        at = [pl.ds(2 * m + n, 128, stride=32) for n in range(2)]
        y = times(long_kin, z_ref[at[0], :], z_ref[at[1], :])
        for n in range(2):
            y_ref[at[n], :] = y_ref[at[n], :] + y[:, 128 * n : 128 * n + 128]
        return 0

    lax.fori_loop(0, 16, second, 0, unroll=4)

    def third(i, _):
        at = pl.ds(pl.multiple_of(i * 128, 128), 128)
        kinetic = y_ref[at, :].T
        damp = damp_ref[:, at]
        v0, v1 = v_ref[0, :, at], v_ref[1, :, at]
        h0 = kinetic[0:48] + coef_ref[:, 0:1] * v0 + coef_ref[:, 2:3] * v1
        h1 = kinetic[48:96] + coef_ref[:, 1:2] * v1 + coef_ref[:, 3:4] * v0
        out_ref[0, :, at] = damp * (2.0 * h0 - damp * prev_ref[0, :, at])
        out_ref[1, :, at] = damp * (2.0 * h1 - damp * prev_ref[1, :, at])
        return 0

    lax.fori_loop(0, 32, third, 0, unroll=4)


SCRATCH = [pltpu.VMEM((4096, 128), F32)] * 2


def local_part(v, prev, coef, damp, radial_long, short_four):
    return pl.pallas_call(
        local_kernel,
        in_specs=[VMEM] * 6,
        out_specs=VMEM,
        out_shape=jax.ShapeDtypeStruct(v.shape, F32),
        scratch_shapes=SCRATCH,
        compiler_params=PARAMS,
        name="local_part",
    )(prev, coef, damp, radial_long, short_four, v)


def next_part(base, pot, prev, coef, damp, radial_long, short_four):
    return pl.pallas_call(
        local_kernel,
        in_specs=[VMEM] * 7,
        out_specs=[VMEM, VMEM],
        out_shape=[jax.ShapeDtypeStruct(base.shape, F32)] * 2,
        scratch_shapes=SCRATCH,
        compiler_params=PARAMS,
        name="next_part",
    )(prev, coef, damp, radial_long, short_four, base, pot)


def add_halo(part, below, above, coef, damp):
    beside = jnp.concatenate([coef[None, :, 4:5] * below, coef[None, :, 5:6] * above], axis=0)
    return part + 2.0 * damp * beside


def last_kernel(part_ref, below_ref, above_ref, pot_ref, coef_ref, damp_ref, out_ref):
    for j in range(pot_ref.shape[0]):
        at = pl.ds(128 * j, 128)
        two_damp = 2.0 * damp_ref[:, at]
        pot0 = pot_ref[j, 0:48, :].astype(F32) + coef_ref[:, 4:5] * below_ref[j]
        pot1 = pot_ref[j, 48:96, :].astype(F32) + coef_ref[:, 5:6] * above_ref[j]
        out_ref[0, :, at] = part_ref[0, :, at] + two_damp * pot0
        out_ref[1, :, at] = part_ref[1, :, at] + two_damp * pot1


def add_last(part, below, above, pot, coef, damp):
    step = 8
    wide = pl.BlockSpec((2, 48, 128 * step), lambda i: (0, 0, i))
    half = pl.BlockSpec((step, 48, 128), lambda i: (i, 0, 0))
    packed = pl.BlockSpec((step, 96, 128), lambda i: (i, 0, 0))
    coefs = pl.BlockSpec((48, 8), lambda i: (0, 0))
    damps = pl.BlockSpec((1, 128 * step), lambda i: (0, i))
    return pl.pallas_call(
        last_kernel,
        grid=(32 // step,),
        in_specs=[wide, half, half, packed, coefs, damps],
        out_specs=wide,
        out_shape=jax.ShapeDtypeStruct(part.shape, F32),
        name="add_last",
    )(part, below, above, pot, coef, damp)


def place(c, y, x, p, i):
    far = 1 if p in (1, 2) else 0
    across = (0, -1, 0, -1, 1, 2, 1, 2)[2 * p + i]
    rows = jnp.where(c == 0, abs(y - far), abs(y - i))
    columns = jnp.where(c == 0, x + across + 4, x + (0, -1, 1, 2)[p] + 4)
    return lax.rem(rows, 2), lax.rem(columns, 4)


def grid_kernel(where_ref, *refs):
    blocks_of, (v_ref, pot_ref, out_ref, x_ref, g_ref, w_ref, o_ref) = refs[:8], refs[8:]
    y, core, x = (where_ref[i] for i in range(3))
    for k in range(2):
        x_ref[:, 128 * k : 128 * k + 128] = v_ref[:, 48 * k : 48 * k + 48, :].reshape(1536, 128)
    g_ref[...] = jnp.zeros_like(g_ref)
    o_ref[...] = jnp.zeros_like(o_ref)
    todo = []
    for n in range(8):
        c = core if n < 4 else 1 - core
        for i in range(2):
            rows, columns = place(c, y, x, n % 4, i)
            todo.append((blocks_of[n], i, 2 * rows + c, columns))
    for ref, i, group, columns in todo:
        part = x_ref[pl.ds(pl.multiple_of(384 * columns, 384), 384), :]
        g_ref[group] = g_ref[group] + dot(ref[i], part)
    for group in range(4):
        pot = pot_ref[:, group].reshape(384, 128)
        weighted = jnp.concatenate([pot, pot], axis=1) * g_ref[group]
        w_ref[group] = weighted.T.astype(BF16)
    for ref, i, group, columns in todo:
        o_ref[columns] = o_ref[columns] + dot(w_ref[group], ref[i])
    for columns in range(4):
        back = o_ref[columns].T.astype(BF16)
        for k in range(2):
            out_ref[8 * columns : 8 * columns + 8, 48 * k : 48 * k + 48, :] = back[
                :, 128 * k : 128 * k + 128
            ].reshape(8, 48, 128)


def on_cells(where, table, v, pot):
    return pl.pallas_call(
        grid_kernel,
        in_specs=[SMEM] + [VMEM] * 10,
        out_specs=VMEM,
        out_shape=jax.ShapeDtypeStruct((32, 96, 128), BF16),
        scratch_shapes=[
            pltpu.VMEM((1536, 256), BF16),
            pltpu.VMEM((4, 384, 256), F32),
            pltpu.VMEM((4, 256, 384), BF16),
            pltpu.VMEM((4, 256, 384), F32),
        ],
        compiler_params=PARAMS,
        name="on_cells",
    )(where, *table, v, pot)


PLANE = ("x", "y_lo", "core")


def plane_permute(value, moves):
    pairs = []
    for x in range(4):
        for y in range(2):
            for c, move in enumerate(moves):
                if move is None:
                    continue
                to_x, to_y = ((x + move) % 4, y) if move else (x, 1 - y)
                pairs.append((4 * x + 2 * y + c, 4 * to_x + 2 * to_y + c))
    return lax.ppermute(value, PLANE, pairs)


def over_z(transform):
    columns = transform.shape[1] // 4
    block = lax.dynamic_slice_in_dim(transform, columns * lax.axis_index("x"), columns, 1)
    block = jnp.broadcast_to(block[None], (8,) + block.shape)
    return lax.all_to_all(block, "z", split_axis=0, concat_axis=0, tiled=True)


def over_plane_first(block):
    block = block.reshape(384, 384)
    one = plane_permute(block, (1, 0))
    two = plane_permute(block, (-1, None))
    three = plane_permute(block, (2, None))
    return jnp.stack([block, one]), jnp.stack([two, three])


def over_plane_second(near, far):
    first = lax.axis_index("core") == 0
    second = plane_permute(near, (0, 1))
    third = plane_permute(jnp.where(first, far, near), (0, -1))
    fourth = plane_permute(near, (None, 2))
    return second, third, fourth


def over_cores(near, far, second, third, fourth):
    first = lax.axis_index("core") == 0
    mine = [near, second, third, jnp.where(first, far, fourth)]
    return mine + [lax.ppermute(pair, "core", [(0, 1), (1, 0)]) for pair in mine]


def regroup(x):
    return lax.all_to_all(x, GRID, split_axis=0, concat_axis=0, tiled=True)


def halos(first, last):
    size = 8
    up = [(i, i + 1) for i in range(size - 1)]
    down = [(j, i) for i, j in up]
    return lax.ppermute(last, HEL, up), lax.ppermute(first, HEL, down)


def coefficients(helicity, band, rotation, coupling):
    first = 2 * lax.axis_index(HEL)
    quantum = band.astype(F32)
    j_term = quantum * (quantum + 1.0)
    k_values = helicity.astype(F32)
    base = jnp.sqrt(jnp.maximum(j_term[:, None] - (k_values * (k_values + 1.0))[None, :], 0.0)) / JMAX
    linked = (helicity[1:] - helicity[:-1] == 1).astype(F32)
    linked = jnp.concatenate([linked, jnp.zeros((1,), F32)])
    coriolis = coupling[:, None] * base * linked[None, :]
    angular = rotation[:, None] * (j_term[:, None] - 2.0 * k_values * k_values) / (JMAX * JMAX)
    padded = jnp.concatenate([jnp.zeros_like(coriolis[:, :1]), coriolis], axis=1)
    part = lax.dynamic_slice_in_dim(padded, first, 3, 1)
    angular = lax.dynamic_slice_in_dim(angular, first, 2, 1)
    return jnp.concatenate(
        [angular, part[:, 1:2], part[:, 1:2], part[:, 0:1], part[:, 2:3], part[:, 0:2]], axis=1
    )


def local(
    phi_prev, phi_curr, helicity, band, rotation, coupling, damping, potential, transform, radial_long, radial_short
):
    where = jnp.stack([lax.axis_index(name) for name in ("y_lo", "core", "x")]).astype(jnp.int32)
    coef = coefficients(helicity, band, rotation, coupling)
    damp = damping.reshape(1, -1)
    cell_damp = lax.dynamic_slice_in_dim(damp, 128 * lax.axis_index(GRID), 128, 1)
    short_four = jnp.kron(jnp.eye(4, dtype=F32), radial_short)
    pot_cells = potential.reshape(8, 4, 48, 128)

    block = over_z(transform)
    sent = pack(phi_curr, BF16)
    ends = (8192.0 * phi_curr).astype(F16)
    first, last = ends[0:1], ends[1:2]
    below, above = halos(first, last)
    v, sent, first, last = lax.optimization_barrier((phi_curr, sent, first, last))
    part = local_part(v, phi_prev, coef, damp, radial_long, short_four)
    sent, block, part = lax.optimization_barrier((sent, block, part))
    by_cells = regroup(sent)
    near, far = over_plane_first(block)
    second = over_plane_second(near, far)
    base = add_halo(part, below.astype(F32) / 8192, above.astype(F32) / 8192, coef, damp)
    sent, second = lax.optimization_barrier((pack(32.0 * base, F16), second))
    base_cells = regroup(sent)
    below, above = halos(sent[:, :48], sent[:, 48:])
    table = over_cores(near, far, *second)
    pot = on_cells(where, table, by_cells, pot_cells)
    next_cells = base_cells.astype(F32) / 32 + 2.0 * cell_damp * pot.astype(F32)
    pot, below, above = lax.optimization_barrier((pot, below, above))
    pot_back = regroup(pot)
    pot_after = on_cells(where, table, next_cells.astype(BF16), pot_cells)
    pot_below, pot_above = halos(pot_back[:, :48], pot_back[:, 48:])
    phi_next, part = next_part(base, pot_back, phi_curr, coef, damp, radial_long, short_four)
    two_damp = 2.0 * damp.reshape(32, 1, 128)
    below = below.astype(F32) / 32 + two_damp * pot_below.astype(F32)
    above = above.astype(F32) / 32 + two_damp * pot_above.astype(F32)
    phi_after = add_last(part, below, above, regroup(pot_after), coef, damp)
    return phi_next, phi_after


def solution(mesh):
    inner = Mesh(mesh.devices.reshape(2, 4, 8, 2, 2), HEL + GRID)
    in_specs = (
        P(HEL, GRID, None),
        P(HEL, GRID, None),
        P(),
        P(GRID),
        P(GRID),
        P(GRID),
        P(),
        P(None, GRID),
        P(GRID, None),
        P(),
        P(),
    )
    out_specs = (P(HEL, GRID, None), P(HEL, GRID, None))
    return jax.shard_map(local, mesh=inner, in_specs=in_specs, out_specs=out_specs, check_vma=False)
```

profile of v0, /device:TPU:24, one launch (start us, length us, event | category | flops | bytes accessed | tf_op | source)
XLA Modules:
  0.0 174.4 jit_solution(9441665010959486332)
XLA Ops:
  0.7 0.9 copy-done
  1.6 0.7 broadcast_in_dim.4
  2.3 8.5 %all-to-all-start = ((bf16[8,48,384]{2,1,0:T(8,128)(2,1)}), bf16[8,48,384]{2,1,0:T(8,128)(2,1)}, u32[]{:S(2)}, u32[]{:S(2)}) async-start(bf16[8,48,384]{2,1,0:T(8,128)(2,1)} %broadcast_in_dim.4), calls=%async_computation | async-start | bytes 589824 | tf_op jit(solution)/shard_map/all_to_all | solution.py:229
  10.8 2.2 %multiply_convert_fusion.1 = (f16[2,48,4096]{2,1,0:T(8,128)(2,1)S(1)}, bf16[2,6,32,8,128]{4,3,2,1,0:T(8,128)(2,1)S(1)}) fusion(f32[2,48,4096]{2,1,0:T(8,128)} %prev_ref.3), kind=kLoop, calls=%fused_computation.4 | loop fusion | flops 1179648 | bytes 3145728 | tf_op jit(solution)/shard_map/convert_element_type | solution.py:295
  13.1 1.0 fusion.7
  14.1 3.4 %collective-permute-start = (f16[1,48,4096]{2,1,0:T(8,128)(2,1)}, f16[1,48,4096]{2,1,0:T(8,128)(2,1)}, u32[]{:S(2)}, u32[]{:S(2)}) collective-permute-start(f16[1,48,4096]{2,1,0:T(8,128)(2,1)} %get-tuple-element.38), channel_id=1, source_target_pairs={{0,32},{32,64},{64,96},{96,128},{128,160},{160,192},{192,224},{1,3... | collective-permute-start | bytes 1179656 | tf_op jit(solution)/shard_map/ppermute | solution.py:262
  17.5 6.1 %collective-permute-start.1 = (f16[1,48,4096]{2,1,0:T(8,128)(2,1)}, f16[1,48,4096]{2,1,0:T(8,128)(2,1)}, u32[]{:S(2)}, u32[]{:S(2)}) collective-permute-start(f16[1,48,4096]{2,1,0:T(8,128)(2,1)} %get-tuple-element.39), channel_id=1, source_target_pairs={{32,0},{64,32},{96,64},{128,96},{160,128},{192,160},{224,192},{33,... | collective-permute-start | bytes 1179656 | tf_op jit(solution)/shard_map/ppermute | solution.py:262
  24.4 1.0 copy.27
  25.4 1.4 copy-done.14
  26.8 8.0 %local_part.1 = f32[2,48,4096]{2,1,0:T(8,128)S(1)} custom-call(f32[2,48,4096]{2,1,0:T(8,128)S(1)} %copy-done.14, f32[48,8]{1,0:T(8,128)S(1)} %copy.20.coef_ref, f32[1,4096]{1,0:T(1,128)S(1)} %bitcast.33, f32[128,128]{1,0:T(8,128)S(1)} %copy-done.18, f32[128,128]{1,0:T(8,128)S(1)} %mul.185.short_ref, f32[2,48,4096]{2,1,0:T(8,128)S(1)} %copy-done.1), custom_call_target="tpu_custom_call" | custom-call | tf_op jit(solution)/shard_map/local_part/pallas_call | solution.py:100
  34.8 0.6 fusion.3
  35.4 1.9 %collective-permute-start.5 = (bf16[384,384]{1,0:T(8,128)(2,1)}, bf16[384,384]{1,0:T(8,128)(2,1)}, u32[]{:S(2)}, u32[]{:S(2)}) collective-permute-start(bf16[384,384]{1,0:T(8,128)(2,1)} %bitcast.9), channel_id=1, source_target_pairs={{0,64},{2,66},{32,96},{34,98},{64,0},{66,2},{96,32},{98,34},{4,68}... | collective-permute-start | bytes 884744 | tf_op jit(solution)/shard_map/ppermute | solution.py:222
  37.3 2.4 %collective-permute-start.4 = (bf16[384,384]{1,0:T(8,128)(2,1)}, bf16[384,384]{1,0:T(8,128)(2,1)}, u32[]{:S(2)}, u32[]{:S(2)}) collective-permute-start(bf16[384,384]{1,0:T(8,128)(2,1)} %bitcast.9), channel_id=1, source_target_pairs={{0,96},{2,98},{32,0},{34,2},{64,32},{66,34},{96,64},{98,66},{4,100... | collective-permute-start | bytes 884744 | tf_op jit(solution)/shard_map/ppermute | solution.py:222
  39.8 1.6 collective-permute-start.2
  41.3 8.9 %all-to-all-start.1 = ((bf16[32,96,128]{2,1,0:T(8,128)(2,1)}), bf16[32,96,128]{2,1,0:T(8,128)(2,1)}, u32[]{:S(2)}, u32[]{:S(2)}) async-start(bf16[32,96,128]{2,1,0:T(8,128)(2,1)} %bitcast.39), calls=%async_computation.1 | async-start | bytes 1572864 | tf_op jit(solution)/shard_map/all_to_all | solution.py:255
  50.2 1.1 convert_multiply_fusion.1
  51.4 1.4 broadcast_select_fusion.1
  52.8 0.7 collective-permute-start.7
  53.9 1.7 collective-permute-start.6
  55.6 1.1 convert_multiply_fusion
  56.7 1.5 fusion.1
  58.2 1.0 copy.26
  59.2 16.2 %collective-permute-done.6.refs_2_ = bf16[2,384,384]{2,1,0:T(8,128)(2,1)} collective-permute-done((bf16[2,384,384]{2,1,0:T(8,128)(2,1)S(1)}, bf16[2,384,384]{2,1,0:T(8,128)(2,1)}, u32[]{:S(2)}, u32[]{:S(2)}) %collective-permute-start.6) | collective-permute-done | bytes 589856 | tf_op jit(solution)/shard_map/ppermute | solution.py:222
  75.5 0.8 copy-done.8
  76.5 7.2 %all-to-all-start.3 = ((f16[32,96,128]{2,1,0:T(8,128)(2,1)}), f16[32,96,128]{2,1,0:T(8,128)(2,1)}, u32[]{:S(2)}, u32[]{:S(2)}) async-start(f16[32,96,128]{2,1,0:T(8,128)(2,1)} %bitcast.35), calls=%async_computation.3 | async-start | bytes 1572864 | tf_op jit(solution)/shard_map/all_to_all | solution.py:255
  84.0 1.1 broadcast_select_fusion.refs_3_
  85.1 0.6 collective-permute-start.11
  86.3 1.1 fusion.6
  87.4 5.0 %collective-permute-start.13 = (f16[32,48,128]{2,1,0:T(8,128)(2,1)}, f16[32,48,128]{2,1,0:T(8,128)(2,1)}, u32[]{:S(2)}, u32[]{:S(2)}) collective-permute-start(f16[32,48,128]{2,1,0:T(8,128)(2,1)} %get-tuple-element.36), channel_id=1, source_target_pairs={{32,0},{64,32},{96,64},{128,96},{160,128},{192,160},{224,192},{33,... | collective-permute-start | bytes 1179656 | tf_op jit(solution)/shard_map/ppermute | solution.py:262
  92.4 0.8 copy-done.11
  93.2 2.1 %collective-permute-start.12 = (f16[32,48,128]{2,1,0:T(8,128)(2,1)}, f16[32,48,128]{2,1,0:T(8,128)(2,1)}, u32[]{:S(2)}, u32[]{:S(2)}) collective-permute-start(f16[32,48,128]{2,1,0:T(8,128)(2,1)} %get-tuple-element.37), channel_id=1, source_target_pairs={{0,32},{32,64},{64,96},{96,128},{128,160},{160,192},{192,224},{1,3... | collective-permute-start | bytes 1179656 | tf_op jit(solution)/shard_map/ppermute | solution.py:262
  95.5 1.1 copy-done.12
  96.5 7.8 %on_cells.2 = bf16[32,96,128]{2,1,0:T(8,128)(2,1)} custom-call(s32[3]{0:T(128)S(1)} %pad_add_fusion.where_ref, bf16[2,384,384]{2,1,0:T(8,128)(2,1)S(1)} %copy-done.4, bf16[2,384,384]{2,1,0:T(8,128)(2,1)S(1)} %copy-done.9, bf16[2,384,384]{2,1,0:T(8,128)(2,1)} %collective-permute-done.6.refs_2_, bf16[2,384,384]{2,1,0:T(8,128)(2,1)S(1)} %broadcast_select_fusion.refs_3_, ...), custom_call_target="tpu_custom_call" | custom-call | tf_op jit(solution)/shard_map/on_cells/pallas_call | solution.py:194
  104.8 5.8 %collective-permute-done.12 = f16[32,48,128]{2,1,0:T(8,128)(2,1)} collective-permute-done((f16[32,48,128]{2,1,0:T(8,128)(2,1)}, f16[32,48,128]{2,1,0:T(8,128)(2,1)}, u32[]{:S(2)}, u32[]{:S(2)}) %collective-permute-start.12) | collective-permute-done | bytes 393248 | tf_op jit(solution)/shard_map/ppermute | solution.py:262
  110.6 7.8 %all-to-all-start.2 = ((bf16[32,96,128]{2,1,0:T(8,128)(2,1)}), bf16[32,96,128]{2,1,0:T(8,128)(2,1)S(1)}, u32[]{:S(2)}, u32[]{:S(2)}) async-start(bf16[32,96,128]{2,1,0:T(8,128)(2,1)} %on_cells.2), calls=%async_computation.2 | async-start | bytes 1572864 | tf_op jit(solution)/shard_map/all_to_all | solution.py:255
  118.6 2.7 %add_convert_fusion.refs_8_ = bf16[32,96,128]{2,1,0:T(8,128)(2,1)} fusion(bf16[32,96,128]{2,1,0:T(8,128)(2,1)} %on_cells.2, f16[32,96,128]{2,1,0:T(8,128)(2,1)} %all-to-all-done.3, f32[128]{0:T(128)S(1)} %dynamic-slice_multiply_fusion), kind=kLoop, calls=%fused_computation.2 | loop fusion | flops 2359296 | bytes 2359808 | tf_op jit(solution)/shard_map/convert_element_type | solution.py:313
  121.3 6.9 %on_cells.3 = bf16[32,96,128]{2,1,0:T(8,128)(2,1)S(1)} custom-call(s32[3]{0:T(128)S(1)} %copy-done.23, bf16[2,384,384]{2,1,0:T(8,128)(2,1)S(1)} %copy-done.4, bf16[2,384,384]{2,1,0:T(8,128)(2,1)S(1)} %copy-done.10, bf16[2,384,384]{2,1,0:T(8,128)(2,1)} %collective-permute-done.6.refs_2_, bf16[2,384,384]{2,1,0:T(8,128)(2,1)S(1)} %copy-done.6, ...), custom_call_target="tpu_custom_call" | custom-call | tf_op jit(solution)/shard_map/on_cells/pallas_call | solution.py:194
  128.2 0.9 copy-done.7
  129.1 12.6 %all-to-all-done.2.refs_1_ = bf16[32,96,128]{2,1,0:T(8,128)(2,1)S(1)} async-done(((bf16[32,96,128]{2,1,0:T(8,128)(2,1)}), bf16[32,96,128]{2,1,0:T(8,128)(2,1)S(1)}, u32[]{:S(2)}, u32[]{:S(2)}) %all-to-all-start.2) | async-done | bytes 786464 | tf_op jit(solution)/shard_map/all_to_all | solution.py:255
  141.8 4.6 %all-to-all-start.4 = ((bf16[32,96,128]{2,1,0:T(8,128)(2,1)}), bf16[32,96,128]{2,1,0:T(8,128)(2,1)}, u32[]{:S(2)}, u32[]{:S(2)}) async-start(bf16[32,96,128]{2,1,0:T(8,128)(2,1)} %copy-done.7), calls=%async_computation.4 | async-start | bytes 1572864 | tf_op jit(solution)/shard_map/all_to_all | solution.py:255
  146.5 3.1 %collective-permute-start.15 = (bf16[32,48,128]{2,1,0:T(8,128)(2,1)S(1)}, bf16[32,48,128]{2,1,0:T(8,128)(2,1)S(1)}, u32[]{:S(2)}, u32[]{:S(2)}) collective-permute-start(bf16[32,48,128]{2,1,0:T(8,128)(2,1)S(1)} %get-tuple-element.34), channel_id=1, source_target_pairs={{32,0},{64,32},{96,64},{128,96},{160,128},{192,160},{224,192},{33,... | collective-permute-start | bytes 1179656 | tf_op jit(solution)/shard_map/ppermute | solution.py:262
  149.6 2.8 %collective-permute-start.14 = (bf16[32,48,128]{2,1,0:T(8,128)(2,1)S(1)}, bf16[32,48,128]{2,1,0:T(8,128)(2,1)S(1)}, u32[]{:S(2)}, u32[]{:S(2)}) collective-permute-start(bf16[32,48,128]{2,1,0:T(8,128)(2,1)S(1)} %get-tuple-element.35), channel_id=1, source_target_pairs={{0,32},{32,64},{64,96},{96,128},{128,160},{160,192},{192,224},{1,3... | collective-permute-start | bytes 1179656 | tf_op jit(solution)/shard_map/ppermute | solution.py:262
  152.5 9.0 %next_part.1 = (f32[2,48,4096]{2,1,0:T(8,128)}, f32[2,48,4096]{2,1,0:T(8,128)S(1)}) custom-call(f32[2,48,4096]{2,1,0:T(8,128)S(1)} %copy-done.1, f32[48,8]{1,0:T(8,128)S(1)} %copy-done.17, f32[1,4096]{1,0:T(1,128)S(1)} %bitcast.34, f32[128,128]{1,0:T(8,128)S(1)} %copy-done.19, f32[128,128]{1,0:T(8,128)S(1)} %mul.185.short_ref, f32[2,48,4096]{2,1,0:T(8,128)S(1)} %copy-done.2, ...), custom_call_target="tpu_custom_call" | custom-call | tf_op jit(solution)/shard_map/next_part/pallas_call | solution.py:112
  161.5 1.2 copy-done.15
  162.7 4.1 %collective-permute-done.14 = bf16[32,48,128]{2,1,0:T(8,128)(2,1)S(1)} collective-permute-done((bf16[32,48,128]{2,1,0:T(8,128)(2,1)S(1)}, bf16[32,48,128]{2,1,0:T(8,128)(2,1)S(1)}, u32[]{:S(2)}, u32[]{:S(2)}) %collective-permute-start.14) | collective-permute-done | bytes 393248 | tf_op jit(solution)/shard_map/ppermute | solution.py:262
  166.8 2.5 %multiply_add_fusion = (f32[32,48,128]{2,1,0:T(8,128)}, f32[32,48,128]{2,1,0:T(8,128)}) fusion(bf16[32,48,128]{2,1,0:T(8,128)(2,1)S(1)} %collective-permute-done.15, f16[32,48,128]{2,1,0:T(8,128)(2,1)} %collective-permute-done.13, f32[32,128]{1,0:T(8,128)S(1)} %copy-done.26, bf16[32,48,128]{2,1,0:T(8,128)(2,1)S(1)} %collective-permute-done.14, ...), kind=kLoop, calls=%fused_computation.8 | loop fusion | flops 1966080 | bytes 3162112 | tf_op jit(solution)/shard_map/add | solution.py:318
  169.3 0.5 all-to-all-done.4.pot_ref
  169.9 4.5 %add_last.1 = f32[2,48,4096]{2,1,0:T(8,128)} custom-call(f32[2,48,4096]{2,1,0:T(8,128)} %copy-done.15, f32[32,48,128]{2,1,0:T(8,128)} %get-tuple-element.43.below_ref, f32[32,48,128]{2,1,0:T(8,128)} %get-tuple-element.42.above_ref, bf16[32,96,128]{2,1,0:T(8,128)(2,1)} %all-to-all-done.4.pot_ref, f32[48,8]{1,0:T(8,128)} %copy-done.16, f32[1,4096]{1,0:T(1,128)} %bitcast.32), custom_call_target="tpu_custom_call" | custom-call | tf_op jit(solution)/shard_map/add_last/pallas_call | solution.py:145
  (96 shorter events, 2.9 us)
Async XLA Ops:
  2.3 33.1 %all-to-all-start = ((bf16[8,48,384]{2,1,0:T(8,128)(2,1)}), bf16[8,48,384]{2,1,0:T(8,128)(2,1)}, u32[]{:S(2)}, u32[]{:S(2)}) async-start(bf16[8,48,384]{2,1,0:T(8,128)(2,1)} %broadcast_in_dim.4), calls=%async_computation | async-start | bytes 589824 | tf_op jit(solution)/shard_map/all_to_all | solution.py:229
  13.0 10.6 %copy-start.31 = (s32[16]{0:T(128)S(1)}, s32[16]{0:T(128)}, u32[]{:S(2)}) copy-start(s32[16]{0:T(128)} %param.13) | copy-start | bytes 196
  13.0 10.7 %copy-start.29 = (s32[48]{0:T(128)S(1)}, s32[48]{0:T(128)}, u32[]{:S(2)}) copy-start(s32[48]{0:T(128)} %param.14) | copy-start | bytes 580
  13.0 10.7 %copy-start.30 = (f32[48]{0:T(128)S(1)}, f32[48]{0:T(128)}, u32[]{:S(2)}) copy-start(f32[48]{0:T(128)} %param.16) | copy-start | bytes 580
  13.0 10.9 %copy-start.28 = (f32[48]{0:T(128)S(1)}, f32[48]{0:T(128)}, u32[]{:S(2)}) copy-start(f32[48]{0:T(128)} %param.15) | copy-start | bytes 580
  13.0 11.1 %copy-start.27 = (f32[32,32]{1,0:T(8,128)S(1)}, f32[32,32]{1,0:T(8,128)}, u32[]{:S(2)}) copy-start(f32[32,32]{1,0:T(8,128)} %param.21) | copy-start | bytes 12292
  13.0 12.4 %copy-start.1 = (f32[2,48,4096]{2,1,0:T(8,128)S(1)}, f32[2,48,4096]{2,1,0:T(8,128)}, u32[]{:S(2)}) copy-start(f32[2,48,4096]{2,1,0:T(8,128)} %prev_ref.3) | copy-start | bytes 4718596
  13.0 12.4 %copy-start.18 = (f32[128,128]{1,0:T(8,128)S(1)}, f32[128,128]{1,0:T(8,128)}, u32[]{:S(2)}) copy-start(f32[128,128]{1,0:T(8,128)} %long_ref.3) | copy-start | bytes 196612
  13.0 12.4 %copy-start.20 = (f32[4096]{0:T(1024)S(1)}, f32[4096]{0:T(1024)}, u32[]{:S(2)}) copy-start(f32[4096]{0:T(1024)} %param.17) | copy-start | bytes 49156
  14.1 36.2 %collective-permute-start = (f16[1,48,4096]{2,1,0:T(8,128)(2,1)}, f16[1,48,4096]{2,1,0:T(8,128)(2,1)}, u32[]{:S(2)}, u32[]{:S(2)}) collective-permute-start(f16[1,48,4096]{2,1,0:T(8,128)(2,1)} %get-tuple-element.38), channel_id=1, source_target_pairs={{0,32},{32,64},{64,96},{96,128},{128,160},{160,192},{192,224},{1,3... | collective-permute-start | bytes 1179656 | tf_op jit(solution)/shard_map/ppermute | solution.py:262
  17.5 38.1 %collective-permute-start.1 = (f16[1,48,4096]{2,1,0:T(8,128)(2,1)}, f16[1,48,4096]{2,1,0:T(8,128)(2,1)}, u32[]{:S(2)}, u32[]{:S(2)}) collective-permute-start(f16[1,48,4096]{2,1,0:T(8,128)(2,1)} %get-tuple-element.39), channel_id=1, source_target_pairs={{32,0},{64,32},{96,64},{128,96},{160,128},{192,160},{224,192},{33,... | collective-permute-start | bytes 1179656 | tf_op jit(solution)/shard_map/ppermute | solution.py:262
  24.1 10.7 %copy-start.16 = (f32[48,8]{1,0:T(8,128)}, f32[48,8]{1,0:T(8,128)S(1)}, u32[]{:S(2)}) copy-start(f32[48,8]{1,0:T(8,128)S(1)} %copy.20.coef_ref) | copy-start | bytes 4612
  25.4 1.4 copy-start.14
  35.4 16.0 %collective-permute-start.5 = (bf16[384,384]{1,0:T(8,128)(2,1)}, bf16[384,384]{1,0:T(8,128)(2,1)}, u32[]{:S(2)}, u32[]{:S(2)}) collective-permute-start(bf16[384,384]{1,0:T(8,128)(2,1)} %bitcast.9), channel_id=1, source_target_pairs={{0,64},{2,66},{32,96},{34,98},{64,0},{66,2},{96,32},{98,34},{4,68}... | collective-permute-start | bytes 884744 | tf_op jit(solution)/shard_map/ppermute | solution.py:222
  37.3 14.0 %collective-permute-start.4 = (bf16[384,384]{1,0:T(8,128)(2,1)}, bf16[384,384]{1,0:T(8,128)(2,1)}, u32[]{:S(2)}, u32[]{:S(2)}) collective-permute-start(bf16[384,384]{1,0:T(8,128)(2,1)} %bitcast.9), channel_id=1, source_target_pairs={{0,96},{2,98},{32,0},{34,2},{64,32},{66,34},{96,64},{98,66},{4,100... | collective-permute-start | bytes 884744 | tf_op jit(solution)/shard_map/ppermute | solution.py:222
  39.8 11.6 %collective-permute-start.2 = (bf16[384,384]{1,0:T(8,128)(2,1)}, bf16[384,384]{1,0:T(8,128)(2,1)}, u32[]{:S(2)}, u32[]{:S(2)}) collective-permute-start(bf16[384,384]{1,0:T(8,128)(2,1)} %bitcast.9), channel_id=1, source_target_pairs={{0,32},{1,3},{2,34},{3,1},{32,64},{33,35},{34,66},{35,33},{64,96},... | collective-permute-start | bytes 884744 | tf_op jit(solution)/shard_map/ppermute | solution.py:222
  41.3 35.1 %all-to-all-start.1 = ((bf16[32,96,128]{2,1,0:T(8,128)(2,1)}), bf16[32,96,128]{2,1,0:T(8,128)(2,1)}, u32[]{:S(2)}, u32[]{:S(2)}) async-start(bf16[32,96,128]{2,1,0:T(8,128)(2,1)} %bitcast.39), calls=%async_computation.1 | async-start | bytes 1572864 | tf_op jit(solution)/shard_map/all_to_all | solution.py:255
  52.8 5.4 %copy-start.3 = (bf16[2,384,384]{2,1,0:T(8,128)(2,1)}, bf16[2,384,384]{2,1,0:T(8,128)(2,1)S(1)}, u32[]{:S(2)}) copy-start(bf16[2,384,384]{2,1,0:T(8,128)(2,1)S(1)} %get-tuple-element.41.refs_0_) | copy-start | bytes 1769476
  52.8 22.7 %collective-permute-start.7 = (bf16[2,384,384]{2,1,0:T(8,128)(2,1)S(1)}, bf16[2,384,384]{2,1,0:T(8,128)(2,1)S(1)}, u32[]{:S(2)}, u32[]{:S(2)}) collective-permute-start(bf16[2,384,384]{2,1,0:T(8,128)(2,1)S(1)} %get-tuple-element.41.refs_0_), channel_id=1, source_target_pairs={{1,65},{3,67},{33,97},{35,99},{65,1},{67,3},{97,33},{99,35},{5,69}... | collective-permute-start | bytes 1769480 | tf_op jit(solution)/shard_map/ppermute | solution.py:222
  53.5 22.0 %collective-permute-start.3 = (bf16[2,384,384]{2,1,0:T(8,128)(2,1)S(1)}, bf16[2,384,384]{2,1,0:T(8,128)(2,1)S(1)}, u32[]{:S(2)}, u32[]{:S(2)}) collective-permute-start(bf16[2,384,384]{2,1,0:T(8,128)(2,1)S(1)} %get-tuple-element.41.refs_0_), channel_id=1, source_target_pairs={{0,2},{1,33},{2,0},{3,35},{32,34},{33,65},{34,32},{35,67},{64,66},... | collective-permute-start | bytes 1769480 | tf_op jit(solution)/shard_map/ppermute | solution.py:222
  53.9 21.6 %collective-permute-start.6 = (bf16[2,384,384]{2,1,0:T(8,128)(2,1)S(1)}, bf16[2,384,384]{2,1,0:T(8,128)(2,1)}, u32[]{:S(2)}, u32[]{:S(2)}) collective-permute-start(bf16[2,384,384]{2,1,0:T(8,128)(2,1)S(1)} %get-tuple-element.40), channel_id=1, source_target_pairs={{0,2},{1,97},{2,0},{3,99},{32,34},{33,1},{34,32},{35,3},{64,66},{6... | collective-permute-start | bytes 1769480 | tf_op jit(solution)/shard_map/ppermute | solution.py:222
  58.2 25.5 %copy-start.4 = (bf16[2,384,384]{2,1,0:T(8,128)(2,1)S(1)}, bf16[2,384,384]{2,1,0:T(8,128)(2,1)}, u32[]{:S(2)}) copy-start(bf16[2,384,384]{2,1,0:T(8,128)(2,1)} %copy-done.3) | copy-start | bytes 1769476
  76.5 9.3 %copy-start.9 = (bf16[2,384,384]{2,1,0:T(8,128)(2,1)S(1)}, bf16[2,384,384]{2,1,0:T(8,128)(2,1)}, u32[]{:S(2)}) copy-start(bf16[2,384,384]{2,1,0:T(8,128)(2,1)} %copy-done.8) | copy-start | bytes 1769476
  76.5 34.1 %all-to-all-start.3 = ((f16[32,96,128]{2,1,0:T(8,128)(2,1)}), f16[32,96,128]{2,1,0:T(8,128)(2,1)}, u32[]{:S(2)}, u32[]{:S(2)}) async-start(f16[32,96,128]{2,1,0:T(8,128)(2,1)} %bitcast.35), calls=%async_computation.3 | async-start | bytes 1572864 | tf_op jit(solution)/shard_map/all_to_all | solution.py:255
  83.7 2.5 %copy-start.24 = (f16[2,6,32,8,128]{4,3,1,0,2:T(8,128)(2,1)S(1)}, f16[2,6,32,8,128]{4,3,1,0,2:T(8,128)(2,1)}, u32[]{:S(2)}) copy-start(f16[2,6,32,8,128]{4,3,1,0,2:T(8,128)(2,1)} %copy.26) | copy-start | bytes 2359300
  83.7 8.7 %collective-permute-start.8 = (bf16[2,384,384]{2,1,0:T(8,128)(2,1)S(1)}, bf16[2,384,384]{2,1,0:T(8,128)(2,1)S(1)}, u32[]{:S(2)}, u32[]{:S(2)}) collective-permute-start(bf16[2,384,384]{2,1,0:T(8,128)(2,1)S(1)} %copy-done.4), channel_id=1, source_target_pairs={{0,1},{1,0},{2,3},{3,2},{4,5},{5,4},{6,7},{7,6},{8,9},{9,8},{10,11... | collective-permute-start | bytes 1769480 | tf_op jit(solution)/shard_map/ppermute | solution.py:251
  85.1 19.2 %copy-start.5 = (bf16[2,384,384]{2,1,0:T(8,128)(2,1)}, bf16[2,384,384]{2,1,0:T(8,128)(2,1)S(1)}, u32[]{:S(2)}) copy-start(bf16[2,384,384]{2,1,0:T(8,128)(2,1)S(1)} %broadcast_select_fusion.refs_3_) | copy-start | bytes 1769476
  85.1 10.3 %collective-permute-start.11 = (bf16[2,384,384]{2,1,0:T(8,128)(2,1)S(1)}, bf16[2,384,384]{2,1,0:T(8,128)(2,1)}, u32[]{:S(2)}, u32[]{:S(2)}) collective-permute-start(bf16[2,384,384]{2,1,0:T(8,128)(2,1)S(1)} %broadcast_select_fusion.refs_3_), channel_id=1, source_target_pairs={{0,1},{1,0},{2,3},{3,2},{4,5},{5,4},{6,7},{7,6},{8,9},{9,8},{10,11... | collective-permute-start | bytes 1769480 | tf_op jit(solution)/shard_map/ppermute | solution.py:251
  85.8 9.7 %collective-permute-start.9 = (bf16[2,384,384]{2,1,0:T(8,128)(2,1)S(1)}, bf16[2,384,384]{2,1,0:T(8,128)(2,1)}, u32[]{:S(2)}, u32[]{:S(2)}) collective-permute-start(bf16[2,384,384]{2,1,0:T(8,128)(2,1)S(1)} %copy-done.9), channel_id=1, source_target_pairs={{0,1},{1,0},{2,3},{3,2},{4,5},{5,4},{6,7},{7,6},{8,9},{9,8},{10,11... | collective-permute-start | bytes 1769480 | tf_op jit(solution)/shard_map/ppermute | solution.py:251
  85.9 9.6 %collective-permute-start.10 = (bf16[2,384,384]{2,1,0:T(8,128)(2,1)}, bf16[2,384,384]{2,1,0:T(8,128)(2,1)}, u32[]{:S(2)}, u32[]{:S(2)}) collective-permute-start(bf16[2,384,384]{2,1,0:T(8,128)(2,1)} %collective-permute-done.6.refs_2_), channel_id=1, source_target_pairs={{0,1},{1,0},{2,3},{3,2},{4,5},{5,4},{6,7},{7,6},{8,9},{9,8},{10,11... | collective-permute-start | bytes 1769480 | tf_op jit(solution)/shard_map/ppermute | solution.py:251
  87.4 17.4 %collective-permute-start.13 = (f16[32,48,128]{2,1,0:T(8,128)(2,1)}, f16[32,48,128]{2,1,0:T(8,128)(2,1)}, u32[]{:S(2)}, u32[]{:S(2)}) collective-permute-start(f16[32,48,128]{2,1,0:T(8,128)(2,1)} %get-tuple-element.36), channel_id=1, source_target_pairs={{32,0},{64,32},{96,64},{128,96},{160,128},{192,160},{224,192},{33,... | collective-permute-start | bytes 1179656 | tf_op jit(solution)/shard_map/ppermute | solution.py:262
  93.2 17.4 %collective-permute-start.12 = (f16[32,48,128]{2,1,0:T(8,128)(2,1)}, f16[32,48,128]{2,1,0:T(8,128)(2,1)}, u32[]{:S(2)}, u32[]{:S(2)}) collective-permute-start(f16[32,48,128]{2,1,0:T(8,128)(2,1)} %get-tuple-element.37), channel_id=1, source_target_pairs={{0,32},{32,64},{64,96},{96,128},{128,160},{160,192},{192,224},{1,3... | collective-permute-start | bytes 1179656 | tf_op jit(solution)/shard_map/ppermute | solution.py:262
  95.4 8.9 %copy-start.22 = (s32[3]{0:T(128)}, s32[3]{0:T(128)S(1)}, u32[]{:S(2)}) copy-start(s32[3]{0:T(128)S(1)} %pad_add_fusion.where_ref) | copy-start | bytes 40
  95.4 1.1 copy-start.12
  104.3 14.2 %copy-start.21 = (f32[4096]{0:T(1024)S(1)}, f32[4096]{0:T(1024)}, u32[]{:S(2)}) copy-start(f32[4096]{0:T(1024)} %param.17) | copy-start | bytes 49156
  110.6 31.2 %all-to-all-start.2 = ((bf16[32,96,128]{2,1,0:T(8,128)(2,1)}), bf16[32,96,128]{2,1,0:T(8,128)(2,1)S(1)}, u32[]{:S(2)}, u32[]{:S(2)}) async-start(bf16[32,96,128]{2,1,0:T(8,128)(2,1)} %on_cells.2), calls=%async_computation.2 | async-start | bytes 1572864 | tf_op jit(solution)/shard_map/all_to_all | solution.py:255
  118.5 2.8 %copy-start.23 = (s32[3]{0:T(128)S(1)}, s32[3]{0:T(128)}, u32[]{:S(2)}) copy-start(s32[3]{0:T(128)} %copy-done.22) | copy-start | bytes 40
  118.5 2.8 %copy-start.6 = (bf16[2,384,384]{2,1,0:T(8,128)(2,1)S(1)}, bf16[2,384,384]{2,1,0:T(8,128)(2,1)}, u32[]{:S(2)}) copy-start(bf16[2,384,384]{2,1,0:T(8,128)(2,1)} %copy-done.5) | copy-start | bytes 1769476
  118.5 2.8 %copy-start.10 = (bf16[2,384,384]{2,1,0:T(8,128)(2,1)S(1)}, bf16[2,384,384]{2,1,0:T(8,128)(2,1)}, u32[]{:S(2)}) copy-start(bf16[2,384,384]{2,1,0:T(8,128)(2,1)} %copy-done.8) | copy-start | bytes 1769476
  118.5 2.8 %copy-start.13 = (bf16[2,384,384]{2,1,0:T(8,128)(2,1)S(1)}, bf16[2,384,384]{2,1,0:T(8,128)(2,1)}, u32[]{:S(2)}) copy-start(bf16[2,384,384]{2,1,0:T(8,128)(2,1)} %copy-done.11) | copy-start | bytes 1769476
  129.1 23.4 %copy-start.17 = (f32[48,8]{1,0:T(8,128)S(1)}, f32[48,8]{1,0:T(8,128)}, u32[]{:S(2)}) copy-start(f32[48,8]{1,0:T(8,128)} %copy-done.16) | copy-start | bytes 4612
  129.1 23.4 %copy-start.19 = (f32[128,128]{1,0:T(8,128)S(1)}, f32[128,128]{1,0:T(8,128)}, u32[]{:S(2)}) copy-start(f32[128,128]{1,0:T(8,128)} %long_ref.3) | copy-start | bytes 196612
  141.8 28.1 %all-to-all-start.4 = ((bf16[32,96,128]{2,1,0:T(8,128)(2,1)}), bf16[32,96,128]{2,1,0:T(8,128)(2,1)}, u32[]{:S(2)}, u32[]{:S(2)}) async-start(bf16[32,96,128]{2,1,0:T(8,128)(2,1)} %copy-done.7), calls=%async_computation.4 | async-start | bytes 1572864 | tf_op jit(solution)/shard_map/all_to_all | solution.py:255
  146.4 6.1 %copy-start.2 = (f32[2,48,4096]{2,1,0:T(8,128)S(1)}, f32[2,48,4096]{2,1,0:T(8,128)}, u32[]{:S(2)}) copy-start(f32[2,48,4096]{2,1,0:T(8,128)} %get-tuple-element.31.refs_0_) | copy-start | bytes 4718596
  146.5 16.2 %collective-permute-start.15 = (bf16[32,48,128]{2,1,0:T(8,128)(2,1)S(1)}, bf16[32,48,128]{2,1,0:T(8,128)(2,1)S(1)}, u32[]{:S(2)}, u32[]{:S(2)}) collective-permute-start(bf16[32,48,128]{2,1,0:T(8,128)(2,1)S(1)} %get-tuple-element.34), channel_id=1, source_target_pairs={{32,0},{64,32},{96,64},{128,96},{160,128},{192,160},{224,192},{33,... | collective-permute-start | bytes 1179656 | tf_op jit(solution)/shard_map/ppermute | solution.py:262
  149.6 17.2 %collective-permute-start.14 = (bf16[32,48,128]{2,1,0:T(8,128)(2,1)S(1)}, bf16[32,48,128]{2,1,0:T(8,128)(2,1)S(1)}, u32[]{:S(2)}, u32[]{:S(2)}) collective-permute-start(bf16[32,48,128]{2,1,0:T(8,128)(2,1)S(1)} %get-tuple-element.35), channel_id=1, source_target_pairs={{0,32},{32,64},{64,96},{96,128},{128,160},{160,192},{192,224},{1,3... | collective-permute-start | bytes 1179656 | tf_op jit(solution)/shard_map/ppermute | solution.py:262
  152.5 14.3 %copy-start.26 = (f32[32,128]{1,0:T(8,128)S(1)}, f32[32,128]{1,0:T(8,128)}, u32[]{:S(2)}) copy-start(f32[32,128]{1,0:T(8,128)} %get-tuple-element.44) | copy-start | bytes 49156
  161.5 1.2 copy-start.15
  (5 other events, 4.5 us)
where the time goes:
time: 176 us; the launch traced here: 174 us
  starting transfers between devices  69.7 us (40%)
  waiting for transfers between devices  39.9 us (23%)
  Pallas kernels  36.1 us (21%)
  other arithmetic  14.9 us (8%)
  local copies, waits for them, and re-layouts  12.7 us (7%)
    all_to_all x4, starting transfers between devices, regroup(): return lax.all_to_all(x, GRID, split_axis=0, concat_axis=0, tiled=True)  28.6 us
    ppermute x6, starting transfers between devices, halos(): return (lax.ppermute(last, HEL, up), lax.ppermute(first, HEL, down))  22.6 us
    ppermute x6, waiting for transfers between devices, plane_permute(): return lax.ppermute(value, PLANE, pairs)  16.3 us
    pallas_call x2, Pallas kernels, on_cells(): pl.pallas_call(grid_kernel, in_specs=[SMEM] + [VMEM] * 10, out_specs=VMEM...  14.7 us
    all_to_all x4, waiting for transfers between devices, regroup(): return lax.all_to_all(x, GRID, split_axis=0, concat_axis=0, tiled=True)  13.2 us
    ppermute x6, waiting for transfers between devices, halos(): return (lax.ppermute(last, HEL, up), lax.ppermute(first, HEL, down))  10.4 us
    pallas_call x1, Pallas kernels, next_part(): pl.pallas_call(local_kernel, in_specs=[VMEM] * 7, out_specs=[VMEM, VMEM],...  8.97 us
    ppermute x6, starting transfers between devices, plane_permute(): return lax.ppermute(value, PLANE, pairs)  8.72 us
  transfers between devices with their start and end apart: 21, of which 6 were waited for; matrix products, arithmetic and copies ran while one was open for 11% of the time, Pallas kernels for 18%

commit v1 on v0

v1 whole, which is shorter than its diff:
```python
import functools
import jax
import jax.numpy as jnp
from jax import lax
from jax.experimental import pallas as pl
from jax.experimental.pallas import tpu as pltpu
from jax.sharding import Mesh, PartitionSpec as P

JMAX = 48
HEL = ("y_hi", "x")
GRID = ("z", "y_lo", "core")
VMEM = pl.BlockSpec(memory_space=pltpu.VMEM)
SMEM = pl.BlockSpec(memory_space=pltpu.SMEM)
PARAMS = pltpu.CompilerParams(vmem_limit_bytes=48 << 20)
F32, BF16, F16 = jnp.float32, jnp.bfloat16, jnp.float16


def split(x):
    high = x.astype(BF16)
    return high, (x - high.astype(F32)).astype(BF16)


def dot(a, b):
    return jnp.dot(a, b, preferred_element_type=F32)


def pack(v):
    return v.reshape(48, 32, 128).transpose(1, 0, 2)


def local_kernel(prev_ref, coef_ref, damp_ref, long_ref, short_ref, *refs):
    if len(refs) == 5:
        (v_ref, out_ref, rounded_ref, z_ref, y_ref), pot_ref = refs, None
    else:
        base_ref, pot_ref, v_ref, out_ref, z_ref, y_ref = refs

    def load(k, j):
        at = pl.ds(pl.multiple_of(j * 128, 128), 128)
        rows = slice(48 * k, 48 * k + 48)
        if pot_ref is None:
            rounded_ref[j, rows, :] = v_ref[k, :, at].astype(BF16)
            return v_ref[k, :, at]
        v = base_ref[j, rows, :] + 2.0 * damp_ref[:, at] * pot_ref[j, rows, :].astype(F32)
        v_ref[k, :, at] = v
        return v

    def halves(matrix):
        high, low = split(0.5 * (matrix + matrix.T))
        top = jnp.concatenate([high, high], axis=1)
        return jnp.concatenate([top, jnp.concatenate([low, jnp.zeros_like(low)], axis=1)], axis=0)

    row, column = (lax.broadcasted_iota(jnp.int32, (128, 128), axis) // 32 for axis in range(2))
    short = jnp.concatenate([short_ref[...]] * 4, axis=1)
    short = jnp.where(row == column, jnp.concatenate([short] * 4, axis=0), 0.0)
    long_kin, short_kin = halves(long_ref[...]), halves(short)
    pad = jnp.zeros((32, 128), F32)

    def times(kin, one, two):
        high, low = split(jnp.concatenate([one, two], axis=1))
        both = dot(kin, jnp.concatenate([high, low], axis=0))
        return both[0:128] + both[128:256]

    def first(i, _):
        z = []
        for n in range(2):
            at = pl.ds(pl.multiple_of(i * 256 + n * 128, 128), 128)
            z.append(jnp.concatenate([load(0, 2 * i + n), load(1, 2 * i + n), pad], axis=0).T)
            z_ref[at, :] = z[n]
        y = times(short_kin, *z)
        for n in range(2):
            at = pl.ds(pl.multiple_of(i * 256 + n * 128, 128), 128)
            y_ref[at, :] = y[:, 128 * n : 128 * n + 128]
        return 0

    lax.fori_loop(0, 16, first, 0, unroll=4)

    def second(m, _):
        at = [pl.ds(2 * m + n, 128, stride=32) for n in range(2)]
        y = times(long_kin, z_ref[at[0], :], z_ref[at[1], :])
        for n in range(2):
            y_ref[at[n], :] = y_ref[at[n], :] + y[:, 128 * n : 128 * n + 128]
        return 0

    lax.fori_loop(0, 16, second, 0, unroll=4)

    def third(i, _):
        at = pl.ds(pl.multiple_of(i * 128, 128), 128)
        kinetic = y_ref[at, :].T
        damp = damp_ref[:, at]
        v0, v1 = v_ref[0, :, at], v_ref[1, :, at]
        h0 = kinetic[0:48] + coef_ref[:, 0:1] * v0 + coef_ref[:, 2:3] * v1
        h1 = kinetic[48:96] + coef_ref[:, 1:2] * v1 + coef_ref[:, 3:4] * v0
        out_ref[i, 0:48, :] = damp * (2.0 * h0 - damp * prev_ref[0, :, at])
        out_ref[i, 48:96, :] = damp * (2.0 * h1 - damp * prev_ref[1, :, at])
        return 0

    lax.fori_loop(0, 32, third, 0, unroll=4)


PACKED = jax.ShapeDtypeStruct((32, 96, 128), F32)
SCRATCH = [pltpu.VMEM((4096, 128), F32)] * 2


def local_part(v, prev, coef, damp, radial_long, radial_short):
    return pl.pallas_call(
        local_kernel,
        in_specs=[VMEM] * 6,
        out_specs=[VMEM, VMEM],
        out_shape=[PACKED, jax.ShapeDtypeStruct(PACKED.shape, BF16)],
        scratch_shapes=SCRATCH,
        compiler_params=PARAMS,
        name="local_part",
    )(prev, coef, damp, radial_long, radial_short, v)


def next_part(base, pot, prev, coef, damp, radial_long, radial_short):
    return pl.pallas_call(
        local_kernel,
        in_specs=[VMEM] * 7,
        out_specs=[VMEM, VMEM],
        out_shape=[jax.ShapeDtypeStruct(prev.shape, F32), PACKED],
        scratch_shapes=SCRATCH,
        compiler_params=PARAMS,
        name="next_part",
    )(prev, coef, damp, radial_long, radial_short, base, pot)


def last_kernel(part_ref, below_ref, above_ref, pot_ref, coef_ref, damp_ref, out_ref):
    for j in range(pot_ref.shape[0]):
        at = pl.ds(128 * j, 128)
        two_damp = 2.0 * damp_ref[:, at]
        pot0 = pot_ref[j, 0:48, :].astype(F32) + coef_ref[:, 4:5] * below_ref[j]
        pot1 = pot_ref[j, 48:96, :].astype(F32) + coef_ref[:, 5:6] * above_ref[j]
        out_ref[0, :, at] = part_ref[j, 0:48, :] + two_damp * pot0
        out_ref[1, :, at] = part_ref[j, 48:96, :] + two_damp * pot1


def add_last(part, below, above, pot, coef, damp):
    step = 8
    wide = pl.BlockSpec((2, 48, 128 * step), lambda i: (0, 0, i))
    half = pl.BlockSpec((step, 48, 128), lambda i: (i, 0, 0))
    packed = pl.BlockSpec((step, 96, 128), lambda i: (i, 0, 0))
    coefs = pl.BlockSpec((48, 8), lambda i: (0, 0))
    damps = pl.BlockSpec((1, 128 * step), lambda i: (0, i))
    return pl.pallas_call(
        last_kernel,
        grid=(32 // step,),
        in_specs=[packed, half, half, packed, coefs, damps],
        out_specs=wide,
        out_shape=jax.ShapeDtypeStruct((2, 48, 4096), F32),
        name="add_last",
    )(part, below, above, pot, coef, damp)


ACROSS = (0, -1, 1, 2)


def grid_kernel(where_ref, own_ref, own_far_ref, other_ref, other_far_ref, v_ref, pot_ref, out_ref, x_ref, w_ref):
    y, core, x = (where_ref[i] for i in range(3))
    owners = [pl.ds(8 * lax.rem(x + across + 4, 4), 8) for across in ACROSS]
    for i, owner in enumerate(owners):
        for k in range(2):
            part = v_ref[owner, 48 * k : 48 * k + 48, :].reshape(384, 128)
            x_ref[384 * i : 384 * i + 384, 128 * k : 128 * k + 128] = part
    halves = (own_ref, own_far_ref), (other_ref, other_far_ref)
    for n, (half, c) in enumerate(zip(halves, (core, 1 - core))):
        for m, (t_ref, rows) in enumerate(zip(half, (y, 1 - y))):
            on_grid = dot(t_ref[...], x_ref[...])
            pot = pot_ref[:, 2 * rows + c].reshape(384, 128)
            weighted = jnp.concatenate([pot, pot], axis=1) * on_grid
            at = 768 * n + 384 * m
            w_ref[:, at : at + 384] = weighted.T.astype(BF16)
    for i, owner in enumerate(owners):
        at = slice(384 * i, 384 * i + 384)
        summed = 0.0
        for n, half in enumerate(halves):
            t = jnp.concatenate([t_ref[:, at] for t_ref in half], axis=0)
            summed = summed + dot(w_ref[:, 768 * n : 768 * n + 768], t)
        back = summed.T.astype(BF16)
        for k in range(2):
            out_ref[owner, 48 * k : 48 * k + 48, :] = back[:, 128 * k : 128 * k + 128].reshape(8, 48, 128)


def on_cells(where, table, v, pot):
    return pl.pallas_call(
        grid_kernel,
        in_specs=[SMEM] + [VMEM] * 6,
        out_specs=VMEM,
        out_shape=jax.ShapeDtypeStruct((32, 96, 128), BF16),
        scratch_shapes=[pltpu.VMEM((1536, 256), BF16), pltpu.VMEM((256, 1536), BF16)],
        compiler_params=PARAMS,
        name="on_cells",
    )(where, *table, v, pot)


def over_z(transform):
    columns = transform.shape[1] // 4
    block = lax.dynamic_slice_in_dim(transform, columns * lax.axis_index("x"), columns, 1)
    block = jnp.broadcast_to(block[None], (8,) + block.shape)
    return lax.all_to_all(block, "z", split_axis=0, concat_axis=0, tiled=True).reshape(-1, columns)


def over_x(block):
    return [lax.ppermute(block, "x", [(i, (i - across) % 4) for i in range(4)]) for across in ACROSS[1:]]


def over_plane(block):
    far = lax.ppermute(block, "y_lo", [(0, 1), (1, 0)])
    own, far, near = lax.optimization_barrier((block, far, over_x(block)))
    mine = jnp.concatenate([own] + near, axis=1)
    others = lax.optimization_barrier(over_x(far))
    mine = [mine, jnp.concatenate([far] + others, axis=1)]
    return mine + [lax.ppermute(rows, "core", [(0, 1), (1, 0)]) for rows in mine]


def regroup(x):
    return lax.all_to_all(x, GRID, split_axis=0, concat_axis=0, tiled=True)


def halos(first, last):
    size = 8
    up = [(i, i + 1) for i in range(size - 1)]
    down = [(j, i) for i, j in up]
    return lax.ppermute(last, HEL, up), lax.ppermute(first, HEL, down)


def coefficients(helicity, band, rotation, coupling):
    first = 2 * lax.axis_index(HEL)
    quantum = band.astype(F32)
    j_term = quantum * (quantum + 1.0)
    k_values = helicity.astype(F32)
    base = jnp.sqrt(jnp.maximum(j_term[:, None] - (k_values * (k_values + 1.0))[None, :], 0.0)) / JMAX
    linked = (helicity[1:] - helicity[:-1] == 1).astype(F32)
    linked = jnp.concatenate([linked, jnp.zeros((1,), F32)])
    coriolis = coupling[:, None] * base * linked[None, :]
    angular = rotation[:, None] * (j_term[:, None] - 2.0 * k_values * k_values) / (JMAX * JMAX)
    padded = jnp.concatenate([jnp.zeros_like(coriolis[:, :1]), coriolis], axis=1)
    part = lax.dynamic_slice_in_dim(padded, first, 3, 1)
    angular = lax.dynamic_slice_in_dim(angular, first, 2, 1)
    return jnp.concatenate(
        [angular, part[:, 1:2], part[:, 1:2], part[:, 0:1], part[:, 2:3], part[:, 0:2]], axis=1
    )


def local(
    phi_prev, phi_curr, helicity, band, rotation, coupling, damping, potential, transform, radial_long, radial_short
):
    where = jnp.stack([lax.axis_index(name) for name in ("y_lo", "core", "x")]).astype(jnp.int32)
    coef = coefficients(helicity, band, rotation, coupling)
    damp = damping.reshape(1, -1)
    cell_damp = lax.dynamic_slice_in_dim(damp, 128 * lax.axis_index(GRID), 128, 1)
    pot_cells = potential.reshape(8, 4, 48, 128)

    two_damp = 2.0 * damp.reshape(32, 1, 128)
    sides = jnp.concatenate([coef[:, 4], coef[:, 5]]).reshape(1, 96, 1)

    first, last = (pack((8192.0 * phi_curr[k]).astype(F16)) for k in range(2))
    below, above = lax.optimization_barrier(halos(first, last))
    block = over_z(transform)
    part, rounded = local_part(phi_curr, phi_prev, coef, damp, radial_long, radial_short)
    beside = jnp.concatenate([below, above], axis=1).astype(F32) / 8192
    sent = jnp.concatenate([(8192.0 * rounded.astype(F32)).astype(F16), (32.0 * (part + two_damp * (sides * beside))).astype(F16)], axis=1)
    sent, part, beside, _ = lax.optimization_barrier((sent, part, beside, block))
    by_cells = regroup(sent)
    base = part + two_damp * (sides * beside)
    table = over_plane(block)
    pot = on_cells(where, table, (by_cells[:, :96].astype(F32) / 8192).astype(BF16), pot_cells)
    next_cells = by_cells[:, 96:].astype(F32) / 32 + 2.0 * cell_damp * pot.astype(F32)
    pot_back = regroup(pot)
    pot_after = on_cells(where, table, next_cells.astype(BF16), pot_cells)
    first, last, pot_after = lax.optimization_barrier((sent[:, 96:144], sent[:, 144:], pot_after))
    below, above = halos(first, last)
    pot_below, pot_above = halos(pot_back[:, :48], pot_back[:, 48:])
    phi_next, part = next_part(base, pot_back, phi_curr, coef, damp, radial_long, radial_short)
    below = below.astype(F32) / 32 + two_damp * pot_below.astype(F32)
    above = above.astype(F32) / 32 + two_damp * pot_above.astype(F32)
    phi_after = add_last(part, below, above, regroup(pot_after), coef, damp)
    return phi_next, phi_after


def solution(mesh):
    inner = Mesh(mesh.devices.reshape(2, 4, 8, 2, 2), HEL + GRID)
    in_specs = (
        P(HEL, GRID, None),
        P(HEL, GRID, None),
        P(),
        P(GRID),
        P(GRID),
        P(GRID),
        P(),
        P(None, GRID),
        P(GRID, None),
        P(),
        P(),
    )
    out_specs = (P(HEL, GRID, None), P(HEL, GRID, None))
    return jax.shard_map(local, mesh=inner, in_specs=in_specs, out_specs=out_specs, check_vma=False)
```

time: 176 us -> 167 us (0.949)
  starting transfers between devices: 69.7 us -> 58.9 us
  waiting for transfers between devices: 39.9 us -> 44.6 us
  Pallas kernels: 36.1 us -> 34.1 us
    all_to_all x4 -> x3, starting transfers between devices: 28.6 us -> 18.6 us  [regroup(): return lax.all_to_all(x, GRID, split_axis=0, concat_axis=0, tiled=True)]
    ppermute x10 -> x9, waiting for transfers between devices: 16.3 us -> 23.5 us  [the longest x6 22.8 us: over_x(): lax.ppermute(block, 'x', [(i, (i - across) % 4) for i in range(4)])]
    ppermute x6, waiting for transfers between devices: 10.4 us -> 3.52 us  [halos(): return (lax.ppermute(last, HEL, up), lax.ppermute(first, HEL, down))]
    all_to_all x4 -> x3, waiting for transfers between devices: 13.2 us -> 17.5 us  [regroup(): return lax.all_to_all(x, GRID, split_axis=0, concat_axis=0, tiled=True)]
    ppermute x10 -> x9, starting transfers between devices: 10.1 us -> 6.78 us  [the longest x6 6.09 us: over_x(): lax.ppermute(block, 'x', [(i, (i - across) % 4) for i in range(4)])]
    div x0 -> x1, other arithmetic: none -> 3.03 us  [local(): beside = jnp.concatenate([below, above], axis=1).astype(F32) / 8192]
    select_n x2 -> x0, other arithmetic: 2.51 us -> none  [the longest x1 1.37 us: over_plane_second(): third = plane_permute(jnp.where(first, far, near), (0, -1))]
    ppermute x6, starting transfers between devices: 22.6 us -> 25 us  [halos(): return (lax.ppermute(last, HEL, up), lax.ppermute(first, HEL, down))]
  transfers between devices with their start and end apart: 21 -> 19, of which waited for: 6 -> 11; matrix products, arithmetic and copies ran while one was open for 11% -> 13% of each run, Pallas kernels for 18% -> 14%
where the time goes in v1:
time: 167 us; the launch traced here: 165 us
  starting transfers between devices  58.9 us (35%)
  waiting for transfers between devices  44.6 us (27%)
  Pallas kernels  34.1 us (20%)
  other arithmetic  13.5 us (8%)
  local copies, waits for them, and re-layouts  12.7 us (8%)
    ppermute x6, starting transfers between devices, halos(): return (lax.ppermute(last, HEL, up), lax.ppermute(first, HEL, down))  25 us
    ppermute x6, waiting for transfers between devices, over_x(): lax.ppermute(block, 'x', [(i, (i - across) % 4) for i in range(4)])  22.8 us
    all_to_all x3, starting transfers between devices, regroup(): return lax.all_to_all(x, GRID, split_axis=0, concat_axis=0, tiled=True)  18.6 us
    all_to_all x3, waiting for transfers between devices, regroup(): return lax.all_to_all(x, GRID, split_axis=0, concat_axis=0, tiled=True)  17.5 us
    pallas_call x2, Pallas kernels, on_cells(): pl.pallas_call(grid_kernel, in_specs=[SMEM] + [VMEM] * 6, out_specs=VMEM,...  12.5 us
    pallas_call x1, Pallas kernels, next_part(): pl.pallas_call(local_kernel, in_specs=[VMEM] * 7, out_specs=[VMEM, VMEM],...  9.22 us
    all_to_all x1, starting transfers between devices, over_z(): lax.all_to_all(block, 'z', split_axis=0, concat_axis=0, tiled=True)  8.47 us
    pallas_call x1, Pallas kernels, local_part(): pl.pallas_call(local_kernel, in_specs=[VMEM] * 6, out_specs=[VMEM, VMEM],...  8.05 us
  transfers between devices with their start and end apart: 19, of which 11 were waited for; matrix products, arithmetic and copies ran while one was open for 13% of the time, Pallas kernels for 14%

profile of v1, /device:TPU:24, one launch (start us, length us, event | category | flops | bytes accessed | tf_op | source)
XLA Modules:
  0.0 164.7 jit_solution(17860276164321410090)
XLA Ops:
  0.7 0.9 copy-done
  1.6 0.7 broadcast_in_dim.2
  2.3 8.5 %all-to-all-start = ((bf16[8,48,384]{2,1,0:T(8,128)(2,1)}), bf16[8,48,384]{2,1,0:T(8,128)(2,1)}, u32[]{:S(2)}, u32[]{:S(2)}) async-start(bf16[8,48,384]{2,1,0:T(8,128)(2,1)} %broadcast_in_dim.2), calls=%async_computation | async-start | bytes 589824 | tf_op jit(solution)/shard_map/all_to_all | solution.py:200
  10.8 1.6 fusion.5
  12.6 0.9 copy.25
  13.5 3.5 %collective-permute-start = (f16[32,48,128]{2,1,0:T(8,128)(2,1)}, f16[32,48,128]{2,1,0:T(8,128)(2,1)}, u32[]{:S(2)}, u32[]{:S(2)}) collective-permute-start(f16[32,48,128]{2,1,0:T(8,128)(2,1)} %bitcast.25), channel_id=1, source_target_pairs={{0,32},{32,64},{64,96},{96,128},{128,160},{160,192},{192,224},{1,3... | collective-permute-start | bytes 1179656 | tf_op jit(solution)/shard_map/ppermute | solution.py:224
  17.2 0.9 copy.24
  18.1 6.0 %collective-permute-start.1 = (f16[32,48,128]{2,1,0:T(8,128)(2,1)}, f16[32,48,128]{2,1,0:T(8,128)(2,1)}, u32[]{:S(2)}, u32[]{:S(2)}) collective-permute-start(f16[32,48,128]{2,1,0:T(8,128)(2,1)} %bitcast.24), channel_id=1, source_target_pairs={{32,0},{64,32},{96,64},{128,96},{160,128},{192,160},{224,192},{33,... | collective-permute-start | bytes 1179656 | tf_op jit(solution)/shard_map/ppermute | solution.py:224
  24.7 8.0 %local_part.1 = (f32[32,96,128]{2,1,0:T(8,128)S(1)}, bf16[32,96,128]{2,1,0:T(8,128)(2,1)S(1)}) custom-call(f32[2,48,4096]{2,1,0:T(8,128)S(1)} %copy-done.8, f32[48,8]{1,0:T(8,128)S(1)} %copy.18.coef_ref, f32[1,4096]{1,0:T(1,128)S(1)} %bitcast.29, f32[128,128]{1,0:T(8,128)S(1)} %copy-done.12, f32[32,32]{1,0:T(8,128)S(1)} %copy-done.13, ...), custom_call_target="tpu_custom_call" | custom-call | tf_op jit(solution)/shard_map/local_part/pallas_call | solution.py:105
  33.1 3.0 %convert_multiply_fusion = (f32[32,96,128]{2,1,0:T(8,128)}, f16[32,96,128]{2,1,0:T(8,128)(2,1)S(1)}) fusion(f16[32,48,128]{2,1,0:T(8,128)(2,1)} %collective-permute-done.1, f16[32,48,128]{2,1,0:T(8,128)(2,1)} %collective-permute-done, f32[32,96,128]{2,1,0:T(8,128)S(1)} %get-tuple-element.26, f32[96]{0:T(128)S(1)} %get-tuple-element.42, ...), kind=kLoop, calls=%fused_computation | loop fusion | flops 3145728 | bytes 4735360 | tf_op jit(solution)/shard_map/div | solution.py:261
  36.1 1.7 %pad_maximum_fusion = f16[32,192,128]{2,1,0:T(8,128)(2,1)} fusion(f16[32,96,128]{2,1,0:T(8,128)(2,1)S(1)} %get-tuple-element.51, f16[32,96,128]{2,1,0:T(8,128)(2,1)S(1)} %multiply_convert_fusion.1), kind=kLoop, calls=%fused_computation.6 | loop fusion | flops 786432 | bytes 3145728 | tf_op jit(solution)/shard_map/concatenate | solution.py:262
  37.8 8.9 %all-to-all-start.1 = ((f16[32,192,128]{2,1,0:T(8,128)(2,1)}), f16[32,192,128]{2,1,0:T(8,128)(2,1)}, u32[]{:S(2)}, u32[]{:S(2)}) async-start(f16[32,192,128]{2,1,0:T(8,128)(2,1)} %pad_maximum_fusion), calls=%async_computation.1 | async-start | bytes 3145728 | tf_op jit(solution)/shard_map/all_to_all | solution.py:217
  46.8 1.1 collective-permute-start.4
  47.9 1.0 collective-permute-start.3
  49.2 9.2 %collective-permute-done.5 = bf16[384,384]{1,0:T(8,128)(2,1)S(1)} collective-permute-done((bf16[384,384]{1,0:T(8,128)(2,1)}, bf16[384,384]{1,0:T(8,128)(2,1)S(1)}, u32[]{:S(2)}, u32[]{:S(2)}) %collective-permute-start.5) | collective-permute-done | bytes 294944 | tf_op jit(solution)/shard_map/ppermute | solution.py:204
  58.4 2.7 %collective-permute-done.4 = bf16[384,384]{1,0:T(8,128)(2,1)S(1)} collective-permute-done((bf16[384,384]{1,0:T(8,128)(2,1)}, bf16[384,384]{1,0:T(8,128)(2,1)S(1)}, u32[]{:S(2)}, u32[]{:S(2)}) %collective-permute-start.4) | collective-permute-done | bytes 294944 | tf_op jit(solution)/shard_map/ppermute | solution.py:204
  61.2 2.7 %collective-permute-done.3 = bf16[384,384]{1,0:T(8,128)(2,1)S(1)} collective-permute-done((bf16[384,384]{1,0:T(8,128)(2,1)}, bf16[384,384]{1,0:T(8,128)(2,1)S(1)}, u32[]{:S(2)}, u32[]{:S(2)}) %collective-permute-start.3) | collective-permute-done | bytes 294944 | tf_op jit(solution)/shard_map/ppermute | solution.py:204
  64.6 1.9 %collective-permute-start.8 = (bf16[384,384]{1,0:T(8,128)(2,1)S(1)}, bf16[384,384]{1,0:T(8,128)(2,1)S(1)}, u32[]{:S(2)}, u32[]{:S(2)}) collective-permute-start(bf16[384,384]{1,0:T(8,128)(2,1)S(1)} %collective-permute-done.2), channel_id=1, source_target_pairs={{0,64},{32,96},{64,0},{96,32},{1,65},{33,97},{65,1},{97,33},{2,66}... | collective-permute-start | bytes 884744 | tf_op jit(solution)/shard_map/ppermute | solution.py:204
  66.5 1.1 collective-permute-start.7
  67.6 0.9 collective-permute-start.6
  68.5 1.7 %constant_dynamic-update-slice_fusion.3 = bf16[384,1536]{1,0:T(8,128)(2,1)} fusion(bf16[384,384]{1,0:T(8,128)(2,1)} %bitcast.6), kind=kLoop, calls=%fused_computation.23 | loop fusion | bytes 589824
  70.2 0.8 constant_dynamic-update-slice_fusion.2
  71.0 0.8 constant_dynamic-update-slice_fusion.1
  71.8 0.8 constant_dynamic-update-slice_fusion.own_ref
  72.6 3.5 %collective-permute-done.8 = bf16[384,384]{1,0:T(8,128)(2,1)S(1)} collective-permute-done((bf16[384,384]{1,0:T(8,128)(2,1)S(1)}, bf16[384,384]{1,0:T(8,128)(2,1)S(1)}, u32[]{:S(2)}, u32[]{:S(2)}) %collective-permute-start.8) | collective-permute-done | bytes 294944 | tf_op jit(solution)/shard_map/ppermute | solution.py:204
  76.1 3.5 %collective-permute-done.7 = bf16[384,384]{1,0:T(8,128)(2,1)S(1)} collective-permute-done((bf16[384,384]{1,0:T(8,128)(2,1)S(1)}, bf16[384,384]{1,0:T(8,128)(2,1)S(1)}, u32[]{:S(2)}, u32[]{:S(2)}) %collective-permute-start.7) | collective-permute-done | bytes 294944 | tf_op jit(solution)/shard_map/ppermute | solution.py:204
  79.6 1.2 collective-permute-done.6
  81.4 4.6 %all-to-all-done.1 = f16[32,192,128]{2,1,0:T(8,128)(2,1)} async-done(((f16[32,192,128]{2,1,0:T(8,128)(2,1)}), f16[32,192,128]{2,1,0:T(8,128)(2,1)}, u32[]{:S(2)}, u32[]{:S(2)}) %all-to-all-start.1) | async-done | bytes 1572896 | tf_op jit(solution)/shard_map/all_to_all | solution.py:217
  86.0 1.4 multiply_convert_fusion.v_ref
  87.4 6.3 %on_cells.2 = bf16[32,96,128]{2,1,0:T(8,128)(2,1)} custom-call(s32[3]{0:T(128)S(1)} %pad_add_fusion.where_ref, bf16[384,1536]{1,0:T(8,128)(2,1)} %constant_dynamic-update-slice_fusion.own_ref, bf16[384,1536]{1,0:T(8,128)(2,1)S(1)} %constant_dynamic-update-slice_fusion.4.own_far_ref, bf16[384,1536]{1,0:T(8,128)(2,1)} %collective-permute-done.9.other_ref, ...), custom_call_target="tpu_custom_call" | custom-call | tf_op jit(solution)/shard_map/on_cells/pallas_call | solution.py:185
  93.7 5.8 %all-to-all-start.2 = ((bf16[32,96,128]{2,1,0:T(8,128)(2,1)}), bf16[32,96,128]{2,1,0:T(8,128)(2,1)S(1)}, u32[]{:S(2)}, u32[]{:S(2)}) async-start(bf16[32,96,128]{2,1,0:T(8,128)(2,1)} %on_cells.2), calls=%async_computation.2 | async-start | bytes 1572864 | tf_op jit(solution)/shard_map/all_to_all | solution.py:217
  99.6 2.1 %fusion.6 = (f16[32,48,128]{2,1,0:T(8,128)(2,1)}, f16[32,48,128]{2,1,0:T(8,128)(2,1)}) fusion(f16[32,192,128]{2,1,0:T(8,128)(2,1)} %pad_maximum_fusion), kind=kLoop, calls=%fused_computation.45 | loop fusion | bytes 1572864 | tf_op jit(solution)/shard_map/slice | solution.py:271
  101.7 1.8 %add_convert_fusion.v_ref = bf16[32,96,128]{2,1,0:T(8,128)(2,1)S(1)} fusion(bf16[32,96,128]{2,1,0:T(8,128)(2,1)} %on_cells.2, f16[32,192,128]{2,1,0:T(8,128)(2,1)} %all-to-all-done.1, f32[128]{0:T(128)S(1)} %dynamic-slice_multiply_fusion), kind=kLoop, calls=%fused_computation.7 | loop fusion | flops 2359296 | bytes 2359808 | tf_op jit(solution)/shard_map/convert_element_type | solution.py:270
  103.7 6.2 %on_cells.3 = bf16[32,96,128]{2,1,0:T(8,128)(2,1)} custom-call(s32[3]{0:T(128)S(1)} %pad_add_fusion.where_ref, bf16[384,1536]{1,0:T(8,128)(2,1)} %constant_dynamic-update-slice_fusion.own_ref, bf16[384,1536]{1,0:T(8,128)(2,1)S(1)} %copy-done.5, bf16[384,1536]{1,0:T(8,128)(2,1)} %collective-permute-done.9.other_ref, ...), custom_call_target="tpu_custom_call" | custom-call | tf_op jit(solution)/shard_map/on_cells/pallas_call | solution.py:185
  109.9 12.9 %all-to-all-done.2.refs_1_ = bf16[32,96,128]{2,1,0:T(8,128)(2,1)S(1)} async-done(((bf16[32,96,128]{2,1,0:T(8,128)(2,1)}), bf16[32,96,128]{2,1,0:T(8,128)(2,1)S(1)}, u32[]{:S(2)}, u32[]{:S(2)}) %all-to-all-start.2) | async-done | bytes 786464 | tf_op jit(solution)/shard_map/all_to_all | solution.py:217
  122.8 4.0 %all-to-all-start.3 = ((bf16[32,96,128]{2,1,0:T(8,128)(2,1)}), bf16[32,96,128]{2,1,0:T(8,128)(2,1)S(1)}, u32[]{:S(2)}, u32[]{:S(2)}) async-start(bf16[32,96,128]{2,1,0:T(8,128)(2,1)} %on_cells.3), calls=%async_computation.3 | async-start | bytes 1572864 | tf_op jit(solution)/shard_map/all_to_all | solution.py:217
  126.8 2.1 %collective-permute-start.11 = (f16[32,48,128]{2,1,0:T(8,128)(2,1)}, f16[32,48,128]{2,1,0:T(8,128)(2,1)S(1)}, u32[]{:S(2)}, u32[]{:S(2)}) collective-permute-start(f16[32,48,128]{2,1,0:T(8,128)(2,1)} %get-tuple-element.39), channel_id=1, source_target_pairs={{0,32},{32,64},{64,96},{96,128},{128,160},{160,192},{192,224},{1,3... | collective-permute-start | bytes 1179656 | tf_op jit(solution)/shard_map/ppermute | solution.py:224
  128.8 7.5 %collective-permute-start.13 = (f16[32,48,128]{2,1,0:T(8,128)(2,1)}, f16[32,48,128]{2,1,0:T(8,128)(2,1)S(1)}, u32[]{:S(2)}, u32[]{:S(2)}) collective-permute-start(f16[32,48,128]{2,1,0:T(8,128)(2,1)} %get-tuple-element.40), channel_id=1, source_target_pairs={{32,0},{64,32},{96,64},{128,96},{160,128},{192,160},{224,192},{33,... | collective-permute-start | bytes 1179656 | tf_op jit(solution)/shard_map/ppermute | solution.py:224
  136.5 2.2 %collective-permute-start.14 = (bf16[32,48,128]{2,1,0:T(8,128)(2,1)S(1)}, bf16[32,48,128]{2,1,0:T(8,128)(2,1)S(1)}, u32[]{:S(2)}, u32[]{:S(2)}) collective-permute-start(bf16[32,48,128]{2,1,0:T(8,128)(2,1)S(1)} %get-tuple-element.48), channel_id=1, source_target_pairs={{32,0},{64,32},{96,64},{128,96},{160,128},{192,160},{224,192},{33,... | collective-permute-start | bytes 1179656 | tf_op jit(solution)/shard_map/ppermute | solution.py:224
  138.7 3.6 %collective-permute-start.12 = (bf16[32,48,128]{2,1,0:T(8,128)(2,1)S(1)}, bf16[32,48,128]{2,1,0:T(8,128)(2,1)S(1)}, u32[]{:S(2)}, u32[]{:S(2)}) collective-permute-start(bf16[32,48,128]{2,1,0:T(8,128)(2,1)S(1)} %get-tuple-element.49), channel_id=1, source_target_pairs={{0,32},{32,64},{64,96},{96,128},{128,160},{160,192},{192,224},{1,3... | collective-permute-start | bytes 1179656 | tf_op jit(solution)/shard_map/ppermute | solution.py:224
  142.3 1.8 %multiply_add_fusion.refs_0_ = f32[32,96,128]{2,1,0:T(8,128)S(1)} fusion(f32[32,96,128]{2,1,0:T(8,128)S(1)} %copy-done.3, f32[32,96,128]{2,1,0:T(8,128)} %get-tuple-element.27, f32[96]{0:T(128)S(1)} %get-tuple-element.43, f32[32,128]{1,0:T(8,128)S(1)} %multiply_bitcast_fusion), kind=kLoop, calls=%fused_computation.9 | loop fusion | flops 1179648 | bytes 4735360 | tf_op jit(solution)/shard_map/add | solution.py:265
  144.1 9.2 %next_part.1 = (f32[2,48,4096]{2,1,0:T(8,128)}, f32[32,96,128]{2,1,0:T(8,128)S(1)}) custom-call(f32[2,48,4096]{2,1,0:T(8,128)S(1)} %copy-done.1, f32[48,8]{1,0:T(8,128)S(1)} %copy.18.coef_ref, f32[1,4096]{1,0:T(1,128)S(1)} %bitcast.30, f32[128,128]{1,0:T(8,128)S(1)} %copy-done.12, f32[32,32]{1,0:T(8,128)S(1)} %copy-done.13, ...), custom_call_target="tpu_custom_call" | custom-call | tf_op jit(solution)/shard_map/next_part/pallas_call | solution.py:117
  153.4 1.2 copy-done.9
  154.5 2.4 %collective-permute-done.14 = bf16[32,48,128]{2,1,0:T(8,128)(2,1)S(1)} collective-permute-done((bf16[32,48,128]{2,1,0:T(8,128)(2,1)S(1)}, bf16[32,48,128]{2,1,0:T(8,128)(2,1)S(1)}, u32[]{:S(2)}, u32[]{:S(2)}) %collective-permute-start.14) | collective-permute-done | bytes 393248 | tf_op jit(solution)/shard_map/ppermute | solution.py:224
  157.0 1.1 collective-permute-done.12
  158.0 1.4 multiply_add_fusion.1
  159.4 0.9 copy-done.14
  160.3 4.4 %add_last.1 = f32[2,48,4096]{2,1,0:T(8,128)} custom-call(f32[32,96,128]{2,1,0:T(8,128)} %copy-done.9, f32[32,48,128]{2,1,0:T(8,128)} %get-tuple-element.53.below_ref, f32[32,48,128]{2,1,0:T(8,128)} %get-tuple-element.52.above_ref, bf16[32,96,128]{2,1,0:T(8,128)(2,1)} %copy-done.14, f32[48,8]{1,0:T(8,128)} %copy-done.10, f32[1,4096]{1,0:T(1,128)} %bitcast.28), custom_call_target="tpu_custom_call" | custom-call | tf_op jit(solution)/shard_map/add_last/pallas_call | solution.py:145
  (73 shorter events, 3.2 us)
Async XLA Ops:
  0.6 0.9 copy-start
  2.3 35.5 %all-to-all-start = ((bf16[8,48,384]{2,1,0:T(8,128)(2,1)}), bf16[8,48,384]{2,1,0:T(8,128)(2,1)}, u32[]{:S(2)}, u32[]{:S(2)}) async-start(bf16[8,48,384]{2,1,0:T(8,128)(2,1)} %broadcast_in_dim.2), calls=%async_computation | async-start | bytes 589824 | tf_op jit(solution)/shard_map/all_to_all | solution.py:200
  12.3 11.8 %copy-start.18 = (s32[16]{0:T(128)S(1)}, s32[16]{0:T(128)}, u32[]{:S(2)}) copy-start(s32[16]{0:T(128)} %param.13) | copy-start | bytes 196
  12.4 11.9 %copy-start.16 = (s32[48]{0:T(128)S(1)}, s32[48]{0:T(128)}, u32[]{:S(2)}) copy-start(s32[48]{0:T(128)} %param.14) | copy-start | bytes 580
  12.4 11.9 %copy-start.17 = (f32[48]{0:T(128)S(1)}, f32[48]{0:T(128)}, u32[]{:S(2)}) copy-start(f32[48]{0:T(128)} %param.16) | copy-start | bytes 580
  12.4 12.0 %copy-start.11 = (f32[4096]{0:T(1024)S(1)}, f32[4096]{0:T(1024)}, u32[]{:S(2)}) copy-start(f32[4096]{0:T(1024)} %param.17) | copy-start | bytes 49156
  12.4 12.1 %copy-start.15 = (f32[48]{0:T(128)S(1)}, f32[48]{0:T(128)}, u32[]{:S(2)}) copy-start(f32[48]{0:T(128)} %param.15) | copy-start | bytes 580
  12.4 12.3 %copy-start.1 = (f32[2,48,4096]{2,1,0:T(8,128)S(1)}, f32[2,48,4096]{2,1,0:T(8,128)}, u32[]{:S(2)}) copy-start(f32[2,48,4096]{2,1,0:T(8,128)} %prev_ref.3) | copy-start | bytes 4718596
  12.4 12.3 %copy-start.8 = (f32[2,48,4096]{2,1,0:T(8,128)S(1)}, f32[2,48,4096]{2,1,0:T(8,128)}, u32[]{:S(2)}) copy-start(f32[2,48,4096]{2,1,0:T(8,128)} %prev_ref.2) | copy-start | bytes 4718596
  12.4 12.3 %copy-start.12 = (f32[128,128]{1,0:T(8,128)S(1)}, f32[128,128]{1,0:T(8,128)}, u32[]{:S(2)}) copy-start(f32[128,128]{1,0:T(8,128)} %long_ref.3) | copy-start | bytes 196612
  12.4 12.3 %copy-start.13 = (f32[32,32]{1,0:T(8,128)S(1)}, f32[32,32]{1,0:T(8,128)}, u32[]{:S(2)}) copy-start(f32[32,32]{1,0:T(8,128)} %short_ref.3) | copy-start | bytes 12292
  13.5 19.6 %collective-permute-start = (f16[32,48,128]{2,1,0:T(8,128)(2,1)}, f16[32,48,128]{2,1,0:T(8,128)(2,1)}, u32[]{:S(2)}, u32[]{:S(2)}) collective-permute-start(f16[32,48,128]{2,1,0:T(8,128)(2,1)} %bitcast.25), channel_id=1, source_target_pairs={{0,32},{32,64},{64,96},{96,128},{128,160},{160,192},{192,224},{1,3... | collective-permute-start | bytes 1179656 | tf_op jit(solution)/shard_map/ppermute | solution.py:224
  18.1 15.0 %collective-permute-start.1 = (f16[32,48,128]{2,1,0:T(8,128)(2,1)}, f16[32,48,128]{2,1,0:T(8,128)(2,1)}, u32[]{:S(2)}, u32[]{:S(2)}) collective-permute-start(f16[32,48,128]{2,1,0:T(8,128)(2,1)} %bitcast.24), channel_id=1, source_target_pairs={{32,0},{64,32},{96,64},{128,96},{160,128},{192,160},{224,192},{33,... | collective-permute-start | bytes 1179656 | tf_op jit(solution)/shard_map/ppermute | solution.py:224
  24.7 119.4 %copy-start.10 = (f32[48,8]{1,0:T(8,128)}, f32[48,8]{1,0:T(8,128)S(1)}, u32[]{:S(2)}) copy-start(f32[48,8]{1,0:T(8,128)S(1)} %copy.18.coef_ref) | copy-start | bytes 4612
  32.8 3.3 %copy-start.2 = (f32[32,96,128]{2,1,0:T(8,128)}, f32[32,96,128]{2,1,0:T(8,128)S(1)}, u32[]{:S(2)}) copy-start(f32[32,96,128]{2,1,0:T(8,128)S(1)} %get-tuple-element.26) | copy-start | bytes 4718596
  37.8 48.1 %all-to-all-start.1 = ((f16[32,192,128]{2,1,0:T(8,128)(2,1)}), f16[32,192,128]{2,1,0:T(8,128)(2,1)}, u32[]{:S(2)}, u32[]{:S(2)}) async-start(f16[32,192,128]{2,1,0:T(8,128)(2,1)} %pad_maximum_fusion), calls=%async_computation.1 | async-start | bytes 3145728 | tf_op jit(solution)/shard_map/all_to_all | solution.py:217
  46.7 11.7 %collective-permute-start.5 = (bf16[384,384]{1,0:T(8,128)(2,1)}, bf16[384,384]{1,0:T(8,128)(2,1)S(1)}, u32[]{:S(2)}, u32[]{:S(2)}) collective-permute-start(bf16[384,384]{1,0:T(8,128)(2,1)} %bitcast.6), channel_id=1, source_target_pairs={{0,64},{32,96},{64,0},{96,32},{1,65},{33,97},{65,1},{97,33},{2,66}... | collective-permute-start | bytes 884744 | tf_op jit(solution)/shard_map/ppermute | solution.py:204
  46.8 14.3 %collective-permute-start.4 = (bf16[384,384]{1,0:T(8,128)(2,1)}, bf16[384,384]{1,0:T(8,128)(2,1)S(1)}, u32[]{:S(2)}, u32[]{:S(2)}) collective-permute-start(bf16[384,384]{1,0:T(8,128)(2,1)} %bitcast.6), channel_id=1, source_target_pairs={{0,96},{32,0},{64,32},{96,64},{1,97},{33,1},{65,33},{97,65},{2,98}... | collective-permute-start | bytes 884744 | tf_op jit(solution)/shard_map/ppermute | solution.py:204
  47.9 16.0 %collective-permute-start.3 = (bf16[384,384]{1,0:T(8,128)(2,1)}, bf16[384,384]{1,0:T(8,128)(2,1)S(1)}, u32[]{:S(2)}, u32[]{:S(2)}) collective-permute-start(bf16[384,384]{1,0:T(8,128)(2,1)} %bitcast.6), channel_id=1, source_target_pairs={{0,32},{32,64},{64,96},{96,0},{1,33},{33,65},{65,97},{97,1},{2,34}... | collective-permute-start | bytes 884744 | tf_op jit(solution)/shard_map/ppermute | solution.py:204
  48.9 15.7 %collective-permute-start.2 = (bf16[384,384]{1,0:T(8,128)(2,1)}, bf16[384,384]{1,0:T(8,128)(2,1)S(1)}, u32[]{:S(2)}, u32[]{:S(2)}) collective-permute-start(bf16[384,384]{1,0:T(8,128)(2,1)} %bitcast.6), channel_id=1, source_target_pairs={{0,2},{2,0},{1,3},{3,1},{4,6},{6,4},{5,7},{7,5},{8,10},{10,8},{9,1... | collective-permute-start | bytes 884744 | tf_op jit(solution)/shard_map/ppermute | solution.py:208
  64.6 11.5 %collective-permute-start.8 = (bf16[384,384]{1,0:T(8,128)(2,1)S(1)}, bf16[384,384]{1,0:T(8,128)(2,1)S(1)}, u32[]{:S(2)}, u32[]{:S(2)}) collective-permute-start(bf16[384,384]{1,0:T(8,128)(2,1)S(1)} %collective-permute-done.2), channel_id=1, source_target_pairs={{0,64},{32,96},{64,0},{96,32},{1,65},{33,97},{65,1},{97,33},{2,66}... | collective-permute-start | bytes 884744 | tf_op jit(solution)/shard_map/ppermute | solution.py:204
  66.5 13.1 %collective-permute-start.7 = (bf16[384,384]{1,0:T(8,128)(2,1)S(1)}, bf16[384,384]{1,0:T(8,128)(2,1)S(1)}, u32[]{:S(2)}, u32[]{:S(2)}) collective-permute-start(bf16[384,384]{1,0:T(8,128)(2,1)S(1)} %collective-permute-done.2), channel_id=1, source_target_pairs={{0,96},{32,0},{64,32},{96,64},{1,97},{33,1},{65,33},{97,65},{2,98}... | collective-permute-start | bytes 884744 | tf_op jit(solution)/shard_map/ppermute | solution.py:204
  67.6 13.2 %collective-permute-start.6 = (bf16[384,384]{1,0:T(8,128)(2,1)S(1)}, bf16[384,384]{1,0:T(8,128)(2,1)S(1)}, u32[]{:S(2)}, u32[]{:S(2)}) collective-permute-start(bf16[384,384]{1,0:T(8,128)(2,1)S(1)} %collective-permute-done.2), channel_id=1, source_target_pairs={{0,32},{32,64},{64,96},{96,0},{1,33},{33,65},{65,97},{97,1},{2,34}... | collective-permute-start | bytes 884744 | tf_op jit(solution)/shard_map/ppermute | solution.py:204
  72.6 14.8 %collective-permute-start.9 = (bf16[384,1536]{1,0:T(8,128)(2,1)}, bf16[384,1536]{1,0:T(8,128)(2,1)}, u32[]{:S(2)}, u32[]{:S(2)}) collective-permute-start(bf16[384,1536]{1,0:T(8,128)(2,1)} %constant_dynamic-update-slice_fusion.own_ref), channel_id=1, source_target_pairs={{0,1},{1,0},{2,3},{3,2},{4,5},{5,4},{6,7},{7,6},{8,9},{9,8},{10,11... | collective-permute-start | bytes 3538952 | tf_op jit(solution)/shard_map/ppermute | solution.py:213
  80.9 12.8 %copy-start.4 = (bf16[384,1536]{1,0:T(8,128)(2,1)}, bf16[384,1536]{1,0:T(8,128)(2,1)S(1)}, u32[]{:S(2)}) copy-start(bf16[384,1536]{1,0:T(8,128)(2,1)S(1)} %constant_dynamic-update-slice_fusion.4.own_far_ref) | copy-start | bytes 3538948
  80.9 6.4 %collective-permute-start.10 = (bf16[384,1536]{1,0:T(8,128)(2,1)S(1)}, bf16[384,1536]{1,0:T(8,128)(2,1)}, u32[]{:S(2)}, u32[]{:S(2)}) collective-permute-start(bf16[384,1536]{1,0:T(8,128)(2,1)S(1)} %constant_dynamic-update-slice_fusion.4.own_far_ref), channel_id=1, source_target_pairs={{0,1},{1,0},{2,3},{3,2},{4,5},{5,4},{6,7},{7,6},{8,9},{9,8},{10,11... | collective-permute-start | bytes 3538952 | tf_op jit(solution)/shard_map/ppermute | solution.py:213
  86.0 1.4 copy-start.6
  93.7 29.1 %all-to-all-start.2 = ((bf16[32,96,128]{2,1,0:T(8,128)(2,1)}), bf16[32,96,128]{2,1,0:T(8,128)(2,1)S(1)}, u32[]{:S(2)}, u32[]{:S(2)}) async-start(bf16[32,96,128]{2,1,0:T(8,128)(2,1)} %on_cells.2), calls=%async_computation.2 | async-start | bytes 1572864 | tf_op jit(solution)/shard_map/all_to_all | solution.py:217
  101.7 1.8 %copy-start.5 = (bf16[384,1536]{1,0:T(8,128)(2,1)S(1)}, bf16[384,1536]{1,0:T(8,128)(2,1)}, u32[]{:S(2)}) copy-start(bf16[384,1536]{1,0:T(8,128)(2,1)} %copy-done.4) | copy-start | bytes 3538948
  101.7 2.0 %copy-start.7 = (f32[1536,128]{1,0:T(8,128)S(1)}, f32[1536,128]{1,0:T(8,128)}, u32[]{:S(2)}) copy-start(f32[1536,128]{1,0:T(8,128)} %param.18) | copy-start | bytes 2359300
  122.8 36.6 %all-to-all-start.3 = ((bf16[32,96,128]{2,1,0:T(8,128)(2,1)}), bf16[32,96,128]{2,1,0:T(8,128)(2,1)S(1)}, u32[]{:S(2)}, u32[]{:S(2)}) async-start(bf16[32,96,128]{2,1,0:T(8,128)(2,1)} %on_cells.3), calls=%async_computation.3 | async-start | bytes 1572864 | tf_op jit(solution)/shard_map/all_to_all | solution.py:217
  126.8 15.5 %copy-start.3 = (f32[32,96,128]{2,1,0:T(8,128)S(1)}, f32[32,96,128]{2,1,0:T(8,128)}, u32[]{:S(2)}) copy-start(f32[32,96,128]{2,1,0:T(8,128)} %copy-done.2) | copy-start | bytes 4718596
  126.8 27.7 %collective-permute-start.11 = (f16[32,48,128]{2,1,0:T(8,128)(2,1)}, f16[32,48,128]{2,1,0:T(8,128)(2,1)S(1)}, u32[]{:S(2)}, u32[]{:S(2)}) collective-permute-start(f16[32,48,128]{2,1,0:T(8,128)(2,1)} %get-tuple-element.39), channel_id=1, source_target_pairs={{0,32},{32,64},{64,96},{96,128},{128,160},{160,192},{192,224},{1,3... | collective-permute-start | bytes 1179656 | tf_op jit(solution)/shard_map/ppermute | solution.py:224
  128.8 25.7 %collective-permute-start.13 = (f16[32,48,128]{2,1,0:T(8,128)(2,1)}, f16[32,48,128]{2,1,0:T(8,128)(2,1)S(1)}, u32[]{:S(2)}, u32[]{:S(2)}) collective-permute-start(f16[32,48,128]{2,1,0:T(8,128)(2,1)} %get-tuple-element.40), channel_id=1, source_target_pairs={{32,0},{64,32},{96,64},{128,96},{160,128},{192,160},{224,192},{33,... | collective-permute-start | bytes 1179656 | tf_op jit(solution)/shard_map/ppermute | solution.py:224
  136.5 20.5 %collective-permute-start.14 = (bf16[32,48,128]{2,1,0:T(8,128)(2,1)S(1)}, bf16[32,48,128]{2,1,0:T(8,128)(2,1)S(1)}, u32[]{:S(2)}, u32[]{:S(2)}) collective-permute-start(bf16[32,48,128]{2,1,0:T(8,128)(2,1)S(1)} %get-tuple-element.48), channel_id=1, source_target_pairs={{32,0},{64,32},{96,64},{128,96},{160,128},{192,160},{224,192},{33,... | collective-permute-start | bytes 1179656 | tf_op jit(solution)/shard_map/ppermute | solution.py:224
  138.7 19.4 %collective-permute-start.12 = (bf16[32,48,128]{2,1,0:T(8,128)(2,1)S(1)}, bf16[32,48,128]{2,1,0:T(8,128)(2,1)S(1)}, u32[]{:S(2)}, u32[]{:S(2)}) collective-permute-start(bf16[32,48,128]{2,1,0:T(8,128)(2,1)S(1)} %get-tuple-element.49), channel_id=1, source_target_pairs={{0,32},{32,64},{64,96},{96,128},{128,160},{160,192},{192,224},{1,3... | collective-permute-start | bytes 1179656 | tf_op jit(solution)/shard_map/ppermute | solution.py:224
  153.4 1.2 copy-start.9
  159.4 0.9 copy-start.14

commit v2 on v1

--- a/solution.py
+++ b/solution.py
@@ -258,18 +258,24 @@
     below, above = lax.optimization_barrier(halos(first, last))
     block = over_z(transform)
     part, rounded = local_part(phi_curr, phi_prev, coef, damp, radial_long, radial_short)
-    beside = jnp.concatenate([below, above], axis=1).astype(F32) / 8192
-    sent = jnp.concatenate([(8192.0 * rounded.astype(F32)).astype(F16), (32.0 * (part + two_damp * (sides * beside))).astype(F16)], axis=1)
-    sent, part, beside, _ = lax.optimization_barrier((sent, part, beside, block))
+    def add_beside(part, below, above):
+        lower = part[:, :48] + two_damp * (sides[:, :48] * (below.astype(F32) / 8192))
+        upper = part[:, 48:] + two_damp * (sides[:, 48:] * (above.astype(F32) / 8192))
+        return lower, upper
+
+    lower, upper = add_beside(part, below, above)
+    sent = [(8192.0 * rounded.astype(F32)).astype(F16), (32.0 * lower).astype(F16), (32.0 * upper).astype(F16)]
+    sent, part, below, above, _ = lax.optimization_barrier((jnp.concatenate(sent, axis=1), part, below, above, block))
     by_cells = regroup(sent)
-    base = part + two_damp * (sides * beside)
+    base = jnp.concatenate(add_beside(part, below, above), axis=1)
     table = over_plane(block)
     pot = on_cells(where, table, (by_cells[:, :96].astype(F32) / 8192).astype(BF16), pot_cells)
     next_cells = by_cells[:, 96:].astype(F32) / 32 + 2.0 * cell_damp * pot.astype(F32)
+    first, last, pot = lax.optimization_barrier((sent[:, 96:144], sent[:, 144:], pot))
     pot_back = regroup(pot)
     pot_after = on_cells(where, table, next_cells.astype(BF16), pot_cells)
-    first, last, pot_after = lax.optimization_barrier((sent[:, 96:144], sent[:, 144:], pot_after))
     below, above = halos(first, last)
+    pot_after, below, above, base = lax.optimization_barrier((pot_after, below, above, base))
     pot_below, pot_above = halos(pot_back[:, :48], pot_back[:, 48:])
     phi_next, part = next_part(base, pot_back, phi_curr, coef, damp, radial_long, radial_short)
     below = below.astype(F32) / 32 + two_damp * pot_below.astype(F32)

time: 167 us -> 164 us (0.982)
  waiting for transfers between devices: 44.6 us -> 33.7 us
  starting transfers between devices: 58.9 us -> 65.4 us
    all_to_all x3, waiting for transfers between devices: 17.5 us -> 2.32 us  [regroup(): return lax.all_to_all(x, GRID, split_axis=0, concat_axis=0, tiled=True)]
    ppermute x6, waiting for transfers between devices: 3.52 us -> 7.96 us  [halos(): return (lax.ppermute(last, HEL, up), lax.ppermute(first, HEL, down))]
    all_to_all x3, starting transfers between devices: 18.6 us -> 23 us  [regroup(): return lax.all_to_all(x, GRID, split_axis=0, concat_axis=0, tiled=True)]
    div x1 -> x0, other arithmetic: 3.03 us -> none  [local(): beside = jnp.concatenate([below, above], axis=1).astype(F32) / 8192]
    ppermute x6, starting transfers between devices: 25 us -> 27.1 us  [halos(): return (lax.ppermute(last, HEL, up), lax.ppermute(first, HEL, down))]
    convert_element_type x0 -> x1, other arithmetic: none -> 1.72 us  [local(): (32.0 * lower).astype(F16)]
    unnamed x46 -> x54, local copies, waits for them, and re-layouts: 6.84 us -> 7.66 us
  transfers between devices with their start and end apart: 19 -> 19, of which waited for: 11 -> 10; matrix products, arithmetic and copies ran while one was open for 13% -> 15% of each run, Pallas kernels for 14% -> 14%
where the time goes in v2:
time: 164 us; the launch traced here: 163 us
  starting transfers between devices  65.4 us (40%)
  Pallas kernels  34 us (21%)
  waiting for transfers between devices  33.7 us (21%)
  other arithmetic  14.7 us (9%)
  local copies, waits for them, and re-layouts  13.6 us (8%)
    ppermute x6, starting transfers between devices, halos(): return (lax.ppermute(last, HEL, up), lax.ppermute(first, HEL, down))  27.1 us
    all_to_all x3, starting transfers between devices, regroup(): return lax.all_to_all(x, GRID, split_axis=0, concat_axis=0, tiled=True)  23 us
    ppermute x6, waiting for transfers between devices, over_x(): lax.ppermute(block, 'x', [(i, (i - across) % 4) for i in range(4)])  22.7 us
    pallas_call x2, Pallas kernels, on_cells(): pl.pallas_call(grid_kernel, in_specs=[SMEM] + [VMEM] * 6, out_specs=VMEM,...  12.4 us
    pallas_call x1, Pallas kernels, next_part(): pl.pallas_call(local_kernel, in_specs=[VMEM] * 7, out_specs=[VMEM, VMEM],...  9.2 us
    all_to_all x1, starting transfers between devices, over_z(): lax.all_to_all(block, 'z', split_axis=0, concat_axis=0, tiled=True)  8.47 us
    pallas_call x1, Pallas kernels, local_part(): pl.pallas_call(local_kernel, in_specs=[VMEM] * 6, out_specs=[VMEM, VMEM],...  8.05 us
    ppermute x6, waiting for transfers between devices, halos(): return (lax.ppermute(last, HEL, up), lax.ppermute(first, HEL, down))  7.96 us
  transfers between devices with their start and end apart: 19, of which 10 were waited for; matrix products, arithmetic and copies ran while one was open for 15% of the time, Pallas kernels for 14%

profile of v2, /device:TPU:24, one launch (start us, length us, event | category | flops | bytes accessed | tf_op | source)
XLA Modules:
  0.0 162.6 jit_solution(4992850501077540338)
XLA Ops:
  0.7 0.9 copy-done
  1.6 0.8 broadcast_in_dim.2
  2.3 8.5 %all-to-all-start = ((bf16[8,48,384]{2,1,0:T(8,128)(2,1)}), bf16[8,48,384]{2,1,0:T(8,128)(2,1)}, u32[]{:S(2)}, u32[]{:S(2)}) async-start(bf16[8,48,384]{2,1,0:T(8,128)(2,1)} %broadcast_in_dim.2), calls=%async_computation | async-start | bytes 589824 | tf_op jit(solution)/shard_map/all_to_all | solution.py:200
  10.8 1.6 fusion.1
  12.6 0.9 copy.25
  13.5 3.5 %collective-permute-start.9 = (f16[32,48,128]{2,1,0:T(8,128)(2,1)}, f16[32,48,128]{2,1,0:T(8,128)(2,1)}, u32[]{:S(2)}, u32[]{:S(2)}) collective-permute-start(f16[32,48,128]{2,1,0:T(8,128)(2,1)} %bitcast.31), channel_id=1, source_target_pairs={{0,32},{32,64},{64,96},{96,128},{128,160},{160,192},{192,224},{1,3... | collective-permute-start | bytes 1179656 | tf_op jit(solution)/shard_map/ppermute | solution.py:224
  17.2 0.9 copy.24
  18.1 6.0 %collective-permute-start.10 = (f16[32,48,128]{2,1,0:T(8,128)(2,1)}, f16[32,48,128]{2,1,0:T(8,128)(2,1)}, u32[]{:S(2)}, u32[]{:S(2)}) collective-permute-start(f16[32,48,128]{2,1,0:T(8,128)(2,1)} %bitcast.30), channel_id=1, source_target_pairs={{32,0},{64,32},{96,64},{128,96},{160,128},{192,160},{224,192},{33,... | collective-permute-start | bytes 1179656 | tf_op jit(solution)/shard_map/ppermute | solution.py:224
  24.8 8.0 %local_part.1 = (f32[32,96,128]{2,1,0:T(8,128)S(1)}, bf16[32,96,128]{2,1,0:T(8,128)(2,1)S(1)}) custom-call(f32[2,48,4096]{2,1,0:T(8,128)S(1)} %copy-done.8, f32[48,8]{1,0:T(8,128)S(1)} %copy.18.coef_ref, f32[1,4096]{1,0:T(1,128)S(1)} %bitcast.35, f32[128,128]{1,0:T(8,128)S(1)} %copy-done.12, f32[32,32]{1,0:T(8,128)S(1)} %copy-done.13, ...), custom_call_target="tpu_custom_call" | custom-call | tf_op jit(solution)/shard_map/local_part/pallas_call | solution.py:105
  33.2 1.7 %multiply_convert_fusion.3 = (f16[32,48,128]{2,1,0:T(8,128)(2,1)S(1)}, f16[32,48,128]{2,1,0:T(8,128)(2,1)S(1)}) fusion(f16[32,48,128]{2,1,0:T(8,128)(2,1)} %collective-permute-done.9, f32[32,96,128]{2,1,0:T(8,128)S(1)} %get-tuple-element.42, f32[48]{0:T(128)S(1)} %get-tuple-element.69, f32[32,128]{1,0:T(8,128)S(1)} %multiply_bitcast_fusion, ...), kind=kLoop, calls=%fused_computation.10 | loop fusion | flops 2359296 | bytes 3162496 | tf_op jit(solution)/shard_map/convert_element_type | solution.py:267
  34.9 1.7 %pad_maximum_fusion = f16[32,192,128]{2,1,0:T(8,128)(2,1)} fusion(f16[32,48,128]{2,1,0:T(8,128)(2,1)S(1)} %get-tuple-element.55, f16[32,48,128]{2,1,0:T(8,128)(2,1)S(1)} %get-tuple-element.54, f16[32,96,128]{2,1,0:T(8,128)(2,1)S(1)} %multiply_convert_fusion.1), kind=kLoop, calls=%fused_computation | loop fusion | flops 1572864 | bytes 3145728 | tf_op jit(solution)/shard_map/concatenate | solution.py:268
  36.7 8.9 %all-to-all-start.1 = ((f16[32,192,128]{2,1,0:T(8,128)(2,1)}), f16[32,192,128]{2,1,0:T(8,128)(2,1)}, u32[]{:S(2)}, u32[]{:S(2)}) async-start(f16[32,192,128]{2,1,0:T(8,128)(2,1)} %pad_maximum_fusion), calls=%async_computation.1 | async-start | bytes 3145728 | tf_op jit(solution)/shard_map/all_to_all | solution.py:217
  45.6 1.1 collective-permute-start.2
  46.7 1.0 collective-permute-start.1
  48.0 9.2 %collective-permute-done.3 = bf16[384,384]{1,0:T(8,128)(2,1)S(1)} collective-permute-done((bf16[384,384]{1,0:T(8,128)(2,1)}, bf16[384,384]{1,0:T(8,128)(2,1)S(1)}, u32[]{:S(2)}, u32[]{:S(2)}) %collective-permute-start.3) | collective-permute-done | bytes 294944 | tf_op jit(solution)/shard_map/ppermute | solution.py:204
  57.2 2.7 %collective-permute-done.2 = bf16[384,384]{1,0:T(8,128)(2,1)S(1)} collective-permute-done((bf16[384,384]{1,0:T(8,128)(2,1)}, bf16[384,384]{1,0:T(8,128)(2,1)S(1)}, u32[]{:S(2)}, u32[]{:S(2)}) %collective-permute-start.2) | collective-permute-done | bytes 294944 | tf_op jit(solution)/shard_map/ppermute | solution.py:204
  60.0 2.7 %collective-permute-done.1 = bf16[384,384]{1,0:T(8,128)(2,1)S(1)} collective-permute-done((bf16[384,384]{1,0:T(8,128)(2,1)}, bf16[384,384]{1,0:T(8,128)(2,1)S(1)}, u32[]{:S(2)}, u32[]{:S(2)}) %collective-permute-start.1) | collective-permute-done | bytes 294944 | tf_op jit(solution)/shard_map/ppermute | solution.py:204
  63.4 1.9 %collective-permute-start.6 = (bf16[384,384]{1,0:T(8,128)(2,1)S(1)}, bf16[384,384]{1,0:T(8,128)(2,1)S(1)}, u32[]{:S(2)}, u32[]{:S(2)}) collective-permute-start(bf16[384,384]{1,0:T(8,128)(2,1)S(1)} %collective-permute-done), channel_id=1, source_target_pairs={{0,64},{32,96},{64,0},{96,32},{1,65},{33,97},{65,1},{97,33},{2,66}... | collective-permute-start | bytes 884744 | tf_op jit(solution)/shard_map/ppermute | solution.py:204
  65.3 1.1 collective-permute-start.5
  66.4 0.9 collective-permute-start.4
  67.3 1.7 %constant_dynamic-update-slice_fusion.3 = bf16[384,1536]{1,0:T(8,128)(2,1)} fusion(bf16[384,384]{1,0:T(8,128)(2,1)} %bitcast.4), kind=kLoop, calls=%fused_computation.20 | loop fusion | bytes 589824
  69.1 0.8 constant_dynamic-update-slice_fusion.2
  69.9 0.8 constant_dynamic-update-slice_fusion.1
  70.7 0.8 constant_dynamic-update-slice_fusion.own_ref
  71.5 3.4 %collective-permute-done.6 = bf16[384,384]{1,0:T(8,128)(2,1)S(1)} collective-permute-done((bf16[384,384]{1,0:T(8,128)(2,1)S(1)}, bf16[384,384]{1,0:T(8,128)(2,1)S(1)}, u32[]{:S(2)}, u32[]{:S(2)}) %collective-permute-start.6) | collective-permute-done | bytes 294944 | tf_op jit(solution)/shard_map/ppermute | solution.py:204
  74.9 3.5 %collective-permute-done.5 = bf16[384,384]{1,0:T(8,128)(2,1)S(1)} collective-permute-done((bf16[384,384]{1,0:T(8,128)(2,1)S(1)}, bf16[384,384]{1,0:T(8,128)(2,1)S(1)}, u32[]{:S(2)}, u32[]{:S(2)}) %collective-permute-start.5) | collective-permute-done | bytes 294944 | tf_op jit(solution)/shard_map/ppermute | solution.py:204
  78.4 1.2 collective-permute-done.4
  80.2 2.3 %fusion.2 = (f16[32,48,128]{2,1,0:T(8,128)(2,1)}, f16[32,48,128]{2,1,0:T(8,128)(2,1)}) fusion(f16[32,192,128]{2,1,0:T(8,128)(2,1)} %pad_maximum_fusion), kind=kLoop, calls=%fused_computation.43 | loop fusion | bytes 1572864 | tf_op jit(solution)/shard_map/slice | solution.py:274
  82.5 2.3 %all-to-all-done.1 = f16[32,192,128]{2,1,0:T(8,128)(2,1)} async-done(((f16[32,192,128]{2,1,0:T(8,128)(2,1)}), f16[32,192,128]{2,1,0:T(8,128)(2,1)}, u32[]{:S(2)}, u32[]{:S(2)}) %all-to-all-start.1) | async-done | bytes 1572896 | tf_op jit(solution)/shard_map/all_to_all | solution.py:217
  84.8 1.4 multiply_convert_fusion.v_ref
  86.2 6.2 %on_cells.2 = bf16[32,96,128]{2,1,0:T(8,128)(2,1)} custom-call(s32[3]{0:T(128)S(1)} %pad_add_fusion.where_ref, bf16[384,1536]{1,0:T(8,128)(2,1)} %constant_dynamic-update-slice_fusion.own_ref, bf16[384,1536]{1,0:T(8,128)(2,1)S(1)} %constant_dynamic-update-slice_fusion.4.own_far_ref, bf16[384,1536]{1,0:T(8,128)(2,1)} %collective-permute-done.7.other_ref, ...), custom_call_target="tpu_custom_call" | custom-call | tf_op jit(solution)/shard_map/on_cells/pallas_call | solution.py:185
  92.4 6.7 %all-to-all-start.2 = ((bf16[32,96,128]{2,1,0:T(8,128)(2,1)}), bf16[32,96,128]{2,1,0:T(8,128)(2,1)S(1)}, u32[]{:S(2)}, u32[]{:S(2)}) async-start(bf16[32,96,128]{2,1,0:T(8,128)(2,1)} %on_cells.2), calls=%async_computation.2 | async-start | bytes 1572864 | tf_op jit(solution)/shard_map/all_to_all | solution.py:217
  99.2 2.0 %multiply_add_fusion.3 = (f32[32,48,128]{2,1,0:T(8,128)S(1)}, f32[32,48,128]{2,1,0:T(8,128)S(1)}) fusion(f16[32,48,128]{2,1,0:T(8,128)(2,1)} %collective-permute-done.9, f32[32,96,128]{2,1,0:T(8,128)} %copy-done.2, f32[48]{0:T(128)S(1)} %get-tuple-element.69, f32[32,128]{1,0:T(8,128)S(1)} %multiply_bitcast_fusion, f32[48]{0:T(128)S(1)} %get-tuple-element.70, ...), kind=kLoop, calls=%fused_computation.8 | loop fusion | flops 1572864 | bytes 3948928 | tf_op jit(solution)/shard_map/add | solution.py:262
  101.2 1.9 %collective-permute-start.11 = (f16[32,48,128]{2,1,0:T(8,128)(2,1)S(1)}, f16[32,48,128]{2,1,0:T(8,128)(2,1)S(1)}, u32[]{:S(2)}, u32[]{:S(2)}) collective-permute-start(f16[32,48,128]{2,1,0:T(8,128)(2,1)S(1)} %copy-done.18), channel_id=1, source_target_pairs={{0,32},{32,64},{64,96},{96,128},{128,160},{160,192},{192,224},{1,3... | collective-permute-start | bytes 1179656 | tf_op jit(solution)/shard_map/ppermute | solution.py:224
  103.1 7.5 %collective-permute-start.12 = (f16[32,48,128]{2,1,0:T(8,128)(2,1)S(1)}, f16[32,48,128]{2,1,0:T(8,128)(2,1)}, u32[]{:S(2)}, u32[]{:S(2)}) collective-permute-start(f16[32,48,128]{2,1,0:T(8,128)(2,1)S(1)} %copy-done.17), channel_id=1, source_target_pairs={{32,0},{64,32},{96,64},{128,96},{160,128},{192,160},{224,192},{33,... | collective-permute-start | bytes 1179656 | tf_op jit(solution)/shard_map/ppermute | solution.py:224
  110.6 1.3 pad_maximum_fusion.1.refs_0_
  112.0 1.8 %add_convert_fusion.v_ref = bf16[32,96,128]{2,1,0:T(8,128)(2,1)S(1)} fusion(bf16[32,96,128]{2,1,0:T(8,128)(2,1)} %on_cells.2, f16[32,192,128]{2,1,0:T(8,128)(2,1)} %all-to-all-done.1, f32[128]{0:T(128)S(1)} %dynamic-slice_multiply_fusion), kind=kLoop, calls=%fused_computation.2 | loop fusion | flops 2359296 | bytes 2359808 | tf_op jit(solution)/shard_map/convert_element_type | solution.py:276
  113.9 6.2 %on_cells.3 = bf16[32,96,128]{2,1,0:T(8,128)(2,1)} custom-call(s32[3]{0:T(128)S(1)} %pad_add_fusion.where_ref, bf16[384,1536]{1,0:T(8,128)(2,1)} %constant_dynamic-update-slice_fusion.own_ref, bf16[384,1536]{1,0:T(8,128)(2,1)S(1)} %copy-done.5, bf16[384,1536]{1,0:T(8,128)(2,1)} %collective-permute-done.7.other_ref, ...), custom_call_target="tpu_custom_call" | custom-call | tf_op jit(solution)/shard_map/on_cells/pallas_call | solution.py:185
  120.1 2.5 %collective-permute-done.11 = f16[32,48,128]{2,1,0:T(8,128)(2,1)S(1)} collective-permute-done((f16[32,48,128]{2,1,0:T(8,128)(2,1)S(1)}, f16[32,48,128]{2,1,0:T(8,128)(2,1)S(1)}, u32[]{:S(2)}, u32[]{:S(2)}) %collective-permute-start.11) | collective-permute-done | bytes 393248 | tf_op jit(solution)/shard_map/ppermute | solution.py:224
  123.3 7.5 %all-to-all-start.3 = ((bf16[32,96,128]{2,1,0:T(8,128)(2,1)}), bf16[32,96,128]{2,1,0:T(8,128)(2,1)S(1)}, u32[]{:S(2)}, u32[]{:S(2)}) async-start(bf16[32,96,128]{2,1,0:T(8,128)(2,1)} %on_cells.3), calls=%async_computation.3 | async-start | bytes 1572864 | tf_op jit(solution)/shard_map/all_to_all | solution.py:217
  130.9 6.1 %collective-permute-start.14 = (bf16[32,48,128]{2,1,0:T(8,128)(2,1)S(1)}, bf16[32,48,128]{2,1,0:T(8,128)(2,1)S(1)}, u32[]{:S(2)}, u32[]{:S(2)}) collective-permute-start(bf16[32,48,128]{2,1,0:T(8,128)(2,1)S(1)} %get-tuple-element.60), channel_id=1, source_target_pairs={{32,0},{64,32},{96,64},{128,96},{160,128},{192,160},{224,192},{33,... | collective-permute-start | bytes 1179656 | tf_op jit(solution)/shard_map/ppermute | solution.py:224
  137.0 2.1 %collective-permute-start.13 = (bf16[32,48,128]{2,1,0:T(8,128)(2,1)S(1)}, bf16[32,48,128]{2,1,0:T(8,128)(2,1)S(1)}, u32[]{:S(2)}, u32[]{:S(2)}) collective-permute-start(bf16[32,48,128]{2,1,0:T(8,128)(2,1)S(1)} %get-tuple-element.61), channel_id=1, source_target_pairs={{0,32},{32,64},{64,96},{96,128},{128,160},{160,192},{192,224},{1,3... | collective-permute-start | bytes 1179656 | tf_op jit(solution)/shard_map/ppermute | solution.py:224
  139.1 9.2 %next_part.1 = (f32[2,48,4096]{2,1,0:T(8,128)}, f32[32,96,128]{2,1,0:T(8,128)S(1)}) custom-call(f32[2,48,4096]{2,1,0:T(8,128)S(1)} %copy-done.1, f32[48,8]{1,0:T(8,128)S(1)} %copy.18.coef_ref, f32[1,4096]{1,0:T(1,128)S(1)} %bitcast.36, f32[128,128]{1,0:T(8,128)S(1)} %copy-done.12, f32[32,32]{1,0:T(8,128)S(1)} %copy-done.13, f32[32,96,128]{2,1,0:T(8,128)S(1)} %copy-done.3, ...), custom_call_target="tpu_custom_call" | custom-call | tf_op jit(solution)/shard_map/next_part/pallas_call | solution.py:117
  148.3 1.2 copy-done.9
  149.4 5.5 %collective-permute-done.13 = bf16[32,48,128]{2,1,0:T(8,128)(2,1)S(1)} collective-permute-done((bf16[32,48,128]{2,1,0:T(8,128)(2,1)S(1)}, bf16[32,48,128]{2,1,0:T(8,128)(2,1)S(1)}, u32[]{:S(2)}, u32[]{:S(2)}) %collective-permute-start.13) | collective-permute-done | bytes 393248 | tf_op jit(solution)/shard_map/ppermute | solution.py:224
  154.9 2.4 %multiply_add_fusion = (f32[32,48,128]{2,1,0:T(8,128)}, f32[32,48,128]{2,1,0:T(8,128)}) fusion(bf16[32,48,128]{2,1,0:T(8,128)(2,1)S(1)} %collective-permute-done.14, f16[32,48,128]{2,1,0:T(8,128)(2,1)} %collective-permute-done.12, f32[32,128]{1,0:T(8,128)S(1)} %multiply_bitcast_fusion, bf16[32,48,128]{2,1,0:T(8,128)(2,1)S(1)} %collective-permute-done.13, ...), kind=kLoop, calls=%fused_computation.5 | loop fusion | flops 1966080 | bytes 3162112 | tf_op jit(solution)/shard_map/add | solution.py:282
  157.3 0.9 copy-done.14
  158.2 4.4 %add_last.1 = f32[2,48,4096]{2,1,0:T(8,128)} custom-call(f32[32,96,128]{2,1,0:T(8,128)} %copy-done.9, f32[32,48,128]{2,1,0:T(8,128)} %get-tuple-element.63.below_ref, f32[32,48,128]{2,1,0:T(8,128)} %get-tuple-element.62.above_ref, bf16[32,96,128]{2,1,0:T(8,128)(2,1)} %copy-done.14, f32[48,8]{1,0:T(8,128)} %copy-done.10, f32[1,4096]{1,0:T(1,128)} %bitcast.34), custom_call_target="tpu_custom_call" | custom-call | tf_op jit(solution)/shard_map/add_last/pallas_call | solution.py:145
  (83 shorter events, 4.0 us)
Async XLA Ops:
  0.6 0.9 copy-start
  2.3 34.3 %all-to-all-start = ((bf16[8,48,384]{2,1,0:T(8,128)(2,1)}), bf16[8,48,384]{2,1,0:T(8,128)(2,1)}, u32[]{:S(2)}, u32[]{:S(2)}) async-start(bf16[8,48,384]{2,1,0:T(8,128)(2,1)} %broadcast_in_dim.2), calls=%async_computation | async-start | bytes 589824 | tf_op jit(solution)/shard_map/all_to_all | solution.py:200
  12.4 11.8 %copy-start.22 = (s32[16]{0:T(128)S(1)}, s32[16]{0:T(128)}, u32[]{:S(2)}) copy-start(s32[16]{0:T(128)} %param.13) | copy-start | bytes 196
  12.4 11.9 %copy-start.20 = (s32[48]{0:T(128)S(1)}, s32[48]{0:T(128)}, u32[]{:S(2)}) copy-start(s32[48]{0:T(128)} %param.14) | copy-start | bytes 580
  12.4 11.9 %copy-start.21 = (f32[48]{0:T(128)S(1)}, f32[48]{0:T(128)}, u32[]{:S(2)}) copy-start(f32[48]{0:T(128)} %param.16) | copy-start | bytes 580
  12.4 12.1 %copy-start.19 = (f32[48]{0:T(128)S(1)}, f32[48]{0:T(128)}, u32[]{:S(2)}) copy-start(f32[48]{0:T(128)} %param.15) | copy-start | bytes 580
  12.4 12.3 %copy-start.1 = (f32[2,48,4096]{2,1,0:T(8,128)S(1)}, f32[2,48,4096]{2,1,0:T(8,128)}, u32[]{:S(2)}) copy-start(f32[2,48,4096]{2,1,0:T(8,128)} %prev_ref.3) | copy-start | bytes 4718596
  12.4 12.3 %copy-start.8 = (f32[2,48,4096]{2,1,0:T(8,128)S(1)}, f32[2,48,4096]{2,1,0:T(8,128)}, u32[]{:S(2)}) copy-start(f32[2,48,4096]{2,1,0:T(8,128)} %prev_ref.2) | copy-start | bytes 4718596
  12.4 12.3 %copy-start.11 = (f32[4096]{0:T(1024)S(1)}, f32[4096]{0:T(1024)}, u32[]{:S(2)}) copy-start(f32[4096]{0:T(1024)} %param.17) | copy-start | bytes 49156
  12.4 12.3 %copy-start.12 = (f32[128,128]{1,0:T(8,128)S(1)}, f32[128,128]{1,0:T(8,128)}, u32[]{:S(2)}) copy-start(f32[128,128]{1,0:T(8,128)} %long_ref.3) | copy-start | bytes 196612
  12.5 12.3 %copy-start.13 = (f32[32,32]{1,0:T(8,128)S(1)}, f32[32,32]{1,0:T(8,128)}, u32[]{:S(2)}) copy-start(f32[32,32]{1,0:T(8,128)} %short_ref.3) | copy-start | bytes 12292
  13.5 19.7 %collective-permute-start.9 = (f16[32,48,128]{2,1,0:T(8,128)(2,1)}, f16[32,48,128]{2,1,0:T(8,128)(2,1)}, u32[]{:S(2)}, u32[]{:S(2)}) collective-permute-start(f16[32,48,128]{2,1,0:T(8,128)(2,1)} %bitcast.31), channel_id=1, source_target_pairs={{0,32},{32,64},{64,96},{96,128},{128,160},{160,192},{192,224},{1,3... | collective-permute-start | bytes 1179656 | tf_op jit(solution)/shard_map/ppermute | solution.py:224
  18.1 15.1 %collective-permute-start.10 = (f16[32,48,128]{2,1,0:T(8,128)(2,1)}, f16[32,48,128]{2,1,0:T(8,128)(2,1)}, u32[]{:S(2)}, u32[]{:S(2)}) collective-permute-start(f16[32,48,128]{2,1,0:T(8,128)(2,1)} %bitcast.30), channel_id=1, source_target_pairs={{32,0},{64,32},{96,64},{128,96},{160,128},{192,160},{224,192},{33,... | collective-permute-start | bytes 1179656 | tf_op jit(solution)/shard_map/ppermute | solution.py:224
  24.7 114.3 %copy-start.10 = (f32[48,8]{1,0:T(8,128)}, f32[48,8]{1,0:T(8,128)S(1)}, u32[]{:S(2)}) copy-start(f32[48,8]{1,0:T(8,128)S(1)} %copy.18.coef_ref) | copy-start | bytes 4612
  32.8 2.1 %copy-start.2 = (f32[32,96,128]{2,1,0:T(8,128)}, f32[32,96,128]{2,1,0:T(8,128)S(1)}, u32[]{:S(2)}) copy-start(f32[32,96,128]{2,1,0:T(8,128)S(1)} %get-tuple-element.42) | copy-start | bytes 4718596
  36.7 48.1 %all-to-all-start.1 = ((f16[32,192,128]{2,1,0:T(8,128)(2,1)}), f16[32,192,128]{2,1,0:T(8,128)(2,1)}, u32[]{:S(2)}, u32[]{:S(2)}) async-start(f16[32,192,128]{2,1,0:T(8,128)(2,1)} %pad_maximum_fusion), calls=%async_computation.1 | async-start | bytes 3145728 | tf_op jit(solution)/shard_map/all_to_all | solution.py:217
  45.5 11.7 %collective-permute-start.3 = (bf16[384,384]{1,0:T(8,128)(2,1)}, bf16[384,384]{1,0:T(8,128)(2,1)S(1)}, u32[]{:S(2)}, u32[]{:S(2)}) collective-permute-start(bf16[384,384]{1,0:T(8,128)(2,1)} %bitcast.4), channel_id=1, source_target_pairs={{0,64},{32,96},{64,0},{96,32},{1,65},{33,97},{65,1},{97,33},{2,66}... | collective-permute-start | bytes 884744 | tf_op jit(solution)/shard_map/ppermute | solution.py:204
  45.6 14.3 %collective-permute-start.2 = (bf16[384,384]{1,0:T(8,128)(2,1)}, bf16[384,384]{1,0:T(8,128)(2,1)S(1)}, u32[]{:S(2)}, u32[]{:S(2)}) collective-permute-start(bf16[384,384]{1,0:T(8,128)(2,1)} %bitcast.4), channel_id=1, source_target_pairs={{0,96},{32,0},{64,32},{96,64},{1,97},{33,1},{65,33},{97,65},{2,98}... | collective-permute-start | bytes 884744 | tf_op jit(solution)/shard_map/ppermute | solution.py:204
  46.7 16.0 %collective-permute-start.1 = (bf16[384,384]{1,0:T(8,128)(2,1)}, bf16[384,384]{1,0:T(8,128)(2,1)S(1)}, u32[]{:S(2)}, u32[]{:S(2)}) collective-permute-start(bf16[384,384]{1,0:T(8,128)(2,1)} %bitcast.4), channel_id=1, source_target_pairs={{0,32},{32,64},{64,96},{96,0},{1,33},{33,65},{65,97},{97,1},{2,34}... | collective-permute-start | bytes 884744 | tf_op jit(solution)/shard_map/ppermute | solution.py:204
  47.7 15.7 %collective-permute-start = (bf16[384,384]{1,0:T(8,128)(2,1)}, bf16[384,384]{1,0:T(8,128)(2,1)S(1)}, u32[]{:S(2)}, u32[]{:S(2)}) collective-permute-start(bf16[384,384]{1,0:T(8,128)(2,1)} %bitcast.4), channel_id=1, source_target_pairs={{0,2},{2,0},{1,3},{3,1},{4,6},{6,4},{5,7},{7,5},{8,10},{10,8},{9,1... | collective-permute-start | bytes 884744 | tf_op jit(solution)/shard_map/ppermute | solution.py:208
  63.4 11.5 %collective-permute-start.6 = (bf16[384,384]{1,0:T(8,128)(2,1)S(1)}, bf16[384,384]{1,0:T(8,128)(2,1)S(1)}, u32[]{:S(2)}, u32[]{:S(2)}) collective-permute-start(bf16[384,384]{1,0:T(8,128)(2,1)S(1)} %collective-permute-done), channel_id=1, source_target_pairs={{0,64},{32,96},{64,0},{96,32},{1,65},{33,97},{65,1},{97,33},{2,66}... | collective-permute-start | bytes 884744 | tf_op jit(solution)/shard_map/ppermute | solution.py:204
  65.3 13.1 %collective-permute-start.5 = (bf16[384,384]{1,0:T(8,128)(2,1)S(1)}, bf16[384,384]{1,0:T(8,128)(2,1)S(1)}, u32[]{:S(2)}, u32[]{:S(2)}) collective-permute-start(bf16[384,384]{1,0:T(8,128)(2,1)S(1)} %collective-permute-done), channel_id=1, source_target_pairs={{0,96},{32,0},{64,32},{96,64},{1,97},{33,1},{65,33},{97,65},{2,98}... | collective-permute-start | bytes 884744 | tf_op jit(solution)/shard_map/ppermute | solution.py:204
  66.4 13.2 %collective-permute-start.4 = (bf16[384,384]{1,0:T(8,128)(2,1)S(1)}, bf16[384,384]{1,0:T(8,128)(2,1)S(1)}, u32[]{:S(2)}, u32[]{:S(2)}) collective-permute-start(bf16[384,384]{1,0:T(8,128)(2,1)S(1)} %collective-permute-done), channel_id=1, source_target_pairs={{0,32},{32,64},{64,96},{96,0},{1,33},{33,65},{65,97},{97,1},{2,34}... | collective-permute-start | bytes 884744 | tf_op jit(solution)/shard_map/ppermute | solution.py:204
  71.5 14.7 %collective-permute-start.7 = (bf16[384,1536]{1,0:T(8,128)(2,1)}, bf16[384,1536]{1,0:T(8,128)(2,1)}, u32[]{:S(2)}, u32[]{:S(2)}) collective-permute-start(bf16[384,1536]{1,0:T(8,128)(2,1)} %constant_dynamic-update-slice_fusion.own_ref), channel_id=1, source_target_pairs={{0,1},{1,0},{2,3},{3,2},{4,5},{5,4},{6,7},{7,6},{8,9},{9,8},{10,11... | collective-permute-start | bytes 3538952 | tf_op jit(solution)/shard_map/ppermute | solution.py:213
  79.7 6.5 %copy-start.4 = (bf16[384,1536]{1,0:T(8,128)(2,1)}, bf16[384,1536]{1,0:T(8,128)(2,1)S(1)}, u32[]{:S(2)}) copy-start(bf16[384,1536]{1,0:T(8,128)(2,1)S(1)} %constant_dynamic-update-slice_fusion.4.own_far_ref) | copy-start | bytes 3538948
  79.8 6.4 %collective-permute-start.8 = (bf16[384,1536]{1,0:T(8,128)(2,1)S(1)}, bf16[384,1536]{1,0:T(8,128)(2,1)}, u32[]{:S(2)}, u32[]{:S(2)}) collective-permute-start(bf16[384,1536]{1,0:T(8,128)(2,1)S(1)} %constant_dynamic-update-slice_fusion.4.own_far_ref), channel_id=1, source_target_pairs={{0,1},{1,0},{2,3},{3,2},{4,5},{5,4},{6,7},{7,6},{8,9},{9,8},{10,11... | collective-permute-start | bytes 3538952 | tf_op jit(solution)/shard_map/ppermute | solution.py:213
  84.8 1.4 copy-start.6
  92.4 30.2 %all-to-all-start.2 = ((bf16[32,96,128]{2,1,0:T(8,128)(2,1)}), bf16[32,96,128]{2,1,0:T(8,128)(2,1)S(1)}, u32[]{:S(2)}, u32[]{:S(2)}) async-start(bf16[32,96,128]{2,1,0:T(8,128)(2,1)} %on_cells.2), calls=%async_computation.2 | async-start | bytes 1572864 | tf_op jit(solution)/shard_map/all_to_all | solution.py:217
  99.2 2.0 %copy-start.18 = (f16[32,48,128]{2,1,0:T(8,128)(2,1)S(1)}, f16[32,48,128]{2,1,0:T(8,128)(2,1)}, u32[]{:S(2)}) copy-start(f16[32,48,128]{2,1,0:T(8,128)(2,1)} %get-tuple-element.40) | copy-start | bytes 1179652
  99.2 3.9 %copy-start.17 = (f16[32,48,128]{2,1,0:T(8,128)(2,1)S(1)}, f16[32,48,128]{2,1,0:T(8,128)(2,1)}, u32[]{:S(2)}) copy-start(f16[32,48,128]{2,1,0:T(8,128)(2,1)} %get-tuple-element.41) | copy-start | bytes 1179652
  101.2 21.4 %collective-permute-start.11 = (f16[32,48,128]{2,1,0:T(8,128)(2,1)S(1)}, f16[32,48,128]{2,1,0:T(8,128)(2,1)S(1)}, u32[]{:S(2)}, u32[]{:S(2)}) collective-permute-start(f16[32,48,128]{2,1,0:T(8,128)(2,1)S(1)} %copy-done.18), channel_id=1, source_target_pairs={{0,32},{32,64},{64,96},{96,128},{128,160},{160,192},{192,224},{1,3... | collective-permute-start | bytes 1179656 | tf_op jit(solution)/shard_map/ppermute | solution.py:224
  103.1 19.5 %collective-permute-start.12 = (f16[32,48,128]{2,1,0:T(8,128)(2,1)S(1)}, f16[32,48,128]{2,1,0:T(8,128)(2,1)}, u32[]{:S(2)}, u32[]{:S(2)}) collective-permute-start(f16[32,48,128]{2,1,0:T(8,128)(2,1)S(1)} %copy-done.17), channel_id=1, source_target_pairs={{32,0},{64,32},{96,64},{128,96},{160,128},{192,160},{224,192},{33,... | collective-permute-start | bytes 1179656 | tf_op jit(solution)/shard_map/ppermute | solution.py:224
  112.0 1.8 %copy-start.5 = (bf16[384,1536]{1,0:T(8,128)(2,1)S(1)}, bf16[384,1536]{1,0:T(8,128)(2,1)}, u32[]{:S(2)}) copy-start(bf16[384,1536]{1,0:T(8,128)(2,1)} %copy-done.4) | copy-start | bytes 3538948
  112.0 2.0 %copy-start.7 = (f32[1536,128]{1,0:T(8,128)S(1)}, f32[1536,128]{1,0:T(8,128)}, u32[]{:S(2)}) copy-start(f32[1536,128]{1,0:T(8,128)} %param.18) | copy-start | bytes 2359300
  122.6 0.8 copy-start.15
  123.3 34.0 %all-to-all-start.3 = ((bf16[32,96,128]{2,1,0:T(8,128)(2,1)}), bf16[32,96,128]{2,1,0:T(8,128)(2,1)S(1)}, u32[]{:S(2)}, u32[]{:S(2)}) async-start(bf16[32,96,128]{2,1,0:T(8,128)(2,1)} %on_cells.3), calls=%async_computation.3 | async-start | bytes 1572864 | tf_op jit(solution)/shard_map/all_to_all | solution.py:217
  130.8 8.2 %copy-start.3 = (f32[32,96,128]{2,1,0:T(8,128)S(1)}, f32[32,96,128]{2,1,0:T(8,128)}, u32[]{:S(2)}) copy-start(f32[32,96,128]{2,1,0:T(8,128)} %pad_maximum_fusion.1.refs_0_) | copy-start | bytes 4718596
  130.9 18.5 %collective-permute-start.14 = (bf16[32,48,128]{2,1,0:T(8,128)(2,1)S(1)}, bf16[32,48,128]{2,1,0:T(8,128)(2,1)S(1)}, u32[]{:S(2)}, u32[]{:S(2)}) collective-permute-start(bf16[32,48,128]{2,1,0:T(8,128)(2,1)S(1)} %get-tuple-element.60), channel_id=1, source_target_pairs={{32,0},{64,32},{96,64},{128,96},{160,128},{192,160},{224,192},{33,... | collective-permute-start | bytes 1179656 | tf_op jit(solution)/shard_map/ppermute | solution.py:224
  137.0 18.0 %copy-start.16 = (f16[32,48,128]{2,1,0:T(8,128)(2,1)S(1)}, f16[32,48,128]{2,1,0:T(8,128)(2,1)}, u32[]{:S(2)}) copy-start(f16[32,48,128]{2,1,0:T(8,128)(2,1)} %copy-done.15) | copy-start | bytes 1179652
  137.0 18.0 %collective-permute-start.13 = (bf16[32,48,128]{2,1,0:T(8,128)(2,1)S(1)}, bf16[32,48,128]{2,1,0:T(8,128)(2,1)S(1)}, u32[]{:S(2)}, u32[]{:S(2)}) collective-permute-start(bf16[32,48,128]{2,1,0:T(8,128)(2,1)S(1)} %get-tuple-element.61), channel_id=1, source_target_pairs={{0,32},{32,64},{64,96},{96,128},{128,160},{160,192},{192,224},{1,3... | collective-permute-start | bytes 1179656 | tf_op jit(solution)/shard_map/ppermute | solution.py:224
  148.3 1.2 copy-start.9
  157.3 0.9 copy-start.14

commit v3 on v2

--- a/solution.py
+++ b/solution.py
@@ -136,7 +136,7 @@
 
 
 def add_last(part, below, above, pot, coef, damp):
-    step = 8
+    step = 16
     wide = pl.BlockSpec((2, 48, 128 * step), lambda i: (0, 0, i))
     half = pl.BlockSpec((step, 48, 128), lambda i: (i, 0, 0))
     packed = pl.BlockSpec((step, 96, 128), lambda i: (i, 0, 0))
@@ -148,6 +148,7 @@
         in_specs=[packed, half, half, packed, coefs, damps],
         out_specs=wide,
         out_shape=jax.ShapeDtypeStruct((2, 48, 4096), F32),
+        compiler_params=PARAMS,
         name="add_last",
     )(part, below, above, pot, coef, damp)
 
@@ -271,10 +272,10 @@
     table = over_plane(block)
     pot = on_cells(where, table, (by_cells[:, :96].astype(F32) / 8192).astype(BF16), pot_cells)
     next_cells = by_cells[:, 96:].astype(F32) / 32 + 2.0 * cell_damp * pot.astype(F32)
-    first, last, pot = lax.optimization_barrier((sent[:, 96:144], sent[:, 144:], pot))
+    sent, pot = lax.optimization_barrier((sent, pot))
     pot_back = regroup(pot)
     pot_after = on_cells(where, table, next_cells.astype(BF16), pot_cells)
-    below, above = halos(first, last)
+    below, above = halos(sent[:, 96:144], sent[:, 144:])
     pot_after, below, above, base = lax.optimization_barrier((pot_after, below, above, base))
     pot_below, pot_above = halos(pot_back[:, :48], pot_back[:, 48:])
     phi_next, part = next_part(base, pot_back, phi_curr, coef, damp, radial_long, radial_short)

time: 164 us -> 160 us (0.976)
  waiting for transfers between devices: 33.7 us -> 40.1 us
  starting transfers between devices: 65.4 us -> 60.4 us
  Pallas kernels: 34 us -> 31.1 us
    ppermute x6, waiting for transfers between devices: 7.96 us -> 12 us  [halos(): return (lax.ppermute(last, HEL, up), lax.ppermute(first, HEL, down))]
    ppermute x6, starting transfers between devices: 27.1 us -> 23.4 us  [halos(): return (lax.ppermute(last, HEL, up), lax.ppermute(first, HEL, down))]
    pallas_call x1, Pallas kernels: 4.37 us -> 1.53 us  [add_last(): pl.pallas_call(last_kernel, grid=(32 // step,), in_specs=[packed, half, h...]
    all_to_all x3, waiting for transfers between devices: 2.32 us -> 4.57 us  [regroup(): return lax.all_to_all(x, GRID, split_axis=0, concat_axis=0, tiled=True)]
    unnamed x54 -> x50, local copies, waits for them, and re-layouts: 7.66 us -> 7.06 us
  transfers between devices with their start and end apart: 19 -> 19, of which waited for: 10 -> 11; matrix products, arithmetic and copies ran while one was open for 15% -> 14% of each run, Pallas kernels for 14% -> 15%
where the time goes in v3:
time: 160 us; the launch traced here: 159 us
  starting transfers between devices  60.4 us (38%)
  waiting for transfers between devices  40.1 us (25%)
  Pallas kernels  31.1 us (19%)
  other arithmetic  14.4 us (9%)
  local copies, waits for them, and re-layouts  12 us (8%)
    ppermute x6, starting transfers between devices, halos(): return (lax.ppermute(last, HEL, up), lax.ppermute(first, HEL, down))  23.4 us
    ppermute x6, waiting for transfers between devices, over_x(): lax.ppermute(block, 'x', [(i, (i - across) % 4) for i in range(4)])  22.8 us
    all_to_all x3, starting transfers between devices, regroup(): return lax.all_to_all(x, GRID, split_axis=0, concat_axis=0, tiled=True)  21.7 us
    pallas_call x2, Pallas kernels, on_cells(): pl.pallas_call(grid_kernel, in_specs=[SMEM] + [VMEM] * 6, out_specs=VMEM,...  12.4 us
    ppermute x6, waiting for transfers between devices, halos(): return (lax.ppermute(last, HEL, up), lax.ppermute(first, HEL, down))  12 us
    pallas_call x1, Pallas kernels, next_part(): pl.pallas_call(local_kernel, in_specs=[VMEM] * 7, out_specs=[VMEM, VMEM],...  9.2 us
    all_to_all x1, starting transfers between devices, over_z(): lax.all_to_all(block, 'z', split_axis=0, concat_axis=0, tiled=True)  8.47 us
    pallas_call x1, Pallas kernels, local_part(): pl.pallas_call(local_kernel, in_specs=[VMEM] * 6, out_specs=[VMEM, VMEM],...  8.05 us
  transfers between devices with their start and end apart: 19, of which 11 were waited for; matrix products, arithmetic and copies ran while one was open for 14% of the time, Pallas kernels for 15%

profile of v3, /device:TPU:24, one launch (start us, length us, event | category | flops | bytes accessed | tf_op | source)
XLA Modules:
  0.0 159.1 jit_solution(2874188202346021534)
XLA Ops:
  0.7 0.9 copy-done
  2.3 8.5 %all-to-all-start = ((bf16[8,48,384]{2,1,0:T(8,128)(2,1)}), bf16[8,48,384]{2,1,0:T(8,128)(2,1)}, u32[]{:S(2)}, u32[]{:S(2)}) async-start(bf16[8,48,384]{2,1,0:T(8,128)(2,1)} %broadcast_in_dim.2), calls=%async_computation | async-start | bytes 589824 | tf_op jit(solution)/shard_map/all_to_all | solution.py:201
  10.7 1.6 fusion.1
  12.6 0.9 copy.25
  13.5 3.5 %collective-permute-start.9 = (f16[32,48,128]{2,1,0:T(8,128)(2,1)}, f16[32,48,128]{2,1,0:T(8,128)(2,1)}, u32[]{:S(2)}, u32[]{:S(2)}) collective-permute-start(f16[32,48,128]{2,1,0:T(8,128)(2,1)} %bitcast.31), channel_id=1, source_target_pairs={{0,32},{32,64},{64,96},{96,128},{128,160},{160,192},{192,224},{1,3... | collective-permute-start | bytes 1179656 | tf_op jit(solution)/shard_map/ppermute | solution.py:225
  17.1 0.9 copy.24
  18.0 6.0 %collective-permute-start.10 = (f16[32,48,128]{2,1,0:T(8,128)(2,1)}, f16[32,48,128]{2,1,0:T(8,128)(2,1)}, u32[]{:S(2)}, u32[]{:S(2)}) collective-permute-start(f16[32,48,128]{2,1,0:T(8,128)(2,1)} %bitcast.30), channel_id=1, source_target_pairs={{32,0},{64,32},{96,64},{128,96},{160,128},{192,160},{224,192},{33,... | collective-permute-start | bytes 1179656 | tf_op jit(solution)/shard_map/ppermute | solution.py:225
  24.7 8.1 %local_part.1 = (f32[32,96,128]{2,1,0:T(8,128)S(1)}, bf16[32,96,128]{2,1,0:T(8,128)(2,1)S(1)}) custom-call(f32[2,48,4096]{2,1,0:T(8,128)S(1)} %copy-done.9, f32[48,8]{1,0:T(8,128)S(1)} %copy.18.coef_ref, f32[1,4096]{1,0:T(1,128)S(1)} %bitcast.34, f32[128,128]{1,0:T(8,128)S(1)} %copy-done.13, f32[32,32]{1,0:T(8,128)S(1)} %copy-done.14, ...), custom_call_target="tpu_custom_call" | custom-call | tf_op jit(solution)/shard_map/local_part/pallas_call | solution.py:105
  33.1 1.7 %multiply_convert_fusion.3 = (f16[32,48,128]{2,1,0:T(8,128)(2,1)S(1)}, f16[32,48,128]{2,1,0:T(8,128)(2,1)S(1)}) fusion(f16[32,48,128]{2,1,0:T(8,128)(2,1)} %collective-permute-done.9, f32[32,96,128]{2,1,0:T(8,128)S(1)} %get-tuple-element.40, f32[48]{0:T(128)S(1)} %get-tuple-element.67, f32[32,128]{1,0:T(8,128)S(1)} %multiply_bitcast_fusion, ...), kind=kLoop, calls=%fused_computation.10 | loop fusion | flops 2359296 | bytes 3162496 | tf_op jit(solution)/shard_map/convert_element_type | solution.py:268
  34.9 1.7 %pad_maximum_fusion = f16[32,192,128]{2,1,0:T(8,128)(2,1)} fusion(f16[32,48,128]{2,1,0:T(8,128)(2,1)S(1)} %get-tuple-element.53, f16[32,48,128]{2,1,0:T(8,128)(2,1)S(1)} %get-tuple-element.52, f16[32,96,128]{2,1,0:T(8,128)(2,1)S(1)} %multiply_convert_fusion.1), kind=kLoop, calls=%fused_computation | loop fusion | flops 1572864 | bytes 3145728 | tf_op jit(solution)/shard_map/concatenate | solution.py:269
  36.6 8.9 %all-to-all-start.1 = ((f16[32,192,128]{2,1,0:T(8,128)(2,1)}), f16[32,192,128]{2,1,0:T(8,128)(2,1)}, u32[]{:S(2)}, u32[]{:S(2)}) async-start(f16[32,192,128]{2,1,0:T(8,128)(2,1)} %pad_maximum_fusion), calls=%async_computation.1 | async-start | bytes 3145728 | tf_op jit(solution)/shard_map/all_to_all | solution.py:218
  45.6 1.1 collective-permute-start.2
  46.7 1.0 collective-permute-start.1
  48.0 9.2 %collective-permute-done.3 = bf16[384,384]{1,0:T(8,128)(2,1)S(1)} collective-permute-done((bf16[384,384]{1,0:T(8,128)(2,1)}, bf16[384,384]{1,0:T(8,128)(2,1)S(1)}, u32[]{:S(2)}, u32[]{:S(2)}) %collective-permute-start.3) | collective-permute-done | bytes 294944 | tf_op jit(solution)/shard_map/ppermute | solution.py:205
  57.2 2.8 %collective-permute-done.2 = bf16[384,384]{1,0:T(8,128)(2,1)S(1)} collective-permute-done((bf16[384,384]{1,0:T(8,128)(2,1)}, bf16[384,384]{1,0:T(8,128)(2,1)S(1)}, u32[]{:S(2)}, u32[]{:S(2)}) %collective-permute-start.2) | collective-permute-done | bytes 294944 | tf_op jit(solution)/shard_map/ppermute | solution.py:205
  60.0 2.7 %collective-permute-done.1 = bf16[384,384]{1,0:T(8,128)(2,1)S(1)} collective-permute-done((bf16[384,384]{1,0:T(8,128)(2,1)}, bf16[384,384]{1,0:T(8,128)(2,1)S(1)}, u32[]{:S(2)}, u32[]{:S(2)}) %collective-permute-start.1) | collective-permute-done | bytes 294944 | tf_op jit(solution)/shard_map/ppermute | solution.py:205
  63.4 1.9 %collective-permute-start.6 = (bf16[384,384]{1,0:T(8,128)(2,1)S(1)}, bf16[384,384]{1,0:T(8,128)(2,1)S(1)}, u32[]{:S(2)}, u32[]{:S(2)}) collective-permute-start(bf16[384,384]{1,0:T(8,128)(2,1)S(1)} %collective-permute-done), channel_id=1, source_target_pairs={{0,64},{32,96},{64,0},{96,32},{1,65},{33,97},{65,1},{97,33},{2,66}... | collective-permute-start | bytes 884744 | tf_op jit(solution)/shard_map/ppermute | solution.py:205
  65.2 1.1 collective-permute-start.5
  66.4 0.9 collective-permute-start.4
  67.3 1.7 %constant_dynamic-update-slice_fusion.3 = bf16[384,1536]{1,0:T(8,128)(2,1)} fusion(bf16[384,384]{1,0:T(8,128)(2,1)} %bitcast.4), kind=kLoop, calls=%fused_computation.20 | loop fusion | bytes 589824
  69.0 0.8 constant_dynamic-update-slice_fusion.2
  69.8 0.8 constant_dynamic-update-slice_fusion.1
  70.6 0.8 constant_dynamic-update-slice_fusion.own_ref
  71.4 3.5 %collective-permute-done.6 = bf16[384,384]{1,0:T(8,128)(2,1)S(1)} collective-permute-done((bf16[384,384]{1,0:T(8,128)(2,1)S(1)}, bf16[384,384]{1,0:T(8,128)(2,1)S(1)}, u32[]{:S(2)}, u32[]{:S(2)}) %collective-permute-start.6) | collective-permute-done | bytes 294944 | tf_op jit(solution)/shard_map/ppermute | solution.py:205
  74.9 3.5 %collective-permute-done.5 = bf16[384,384]{1,0:T(8,128)(2,1)S(1)} collective-permute-done((bf16[384,384]{1,0:T(8,128)(2,1)S(1)}, bf16[384,384]{1,0:T(8,128)(2,1)S(1)}, u32[]{:S(2)}, u32[]{:S(2)}) %collective-permute-start.5) | collective-permute-done | bytes 294944 | tf_op jit(solution)/shard_map/ppermute | solution.py:205
  78.4 1.1 collective-permute-done.4
  80.2 4.6 %all-to-all-done.1 = f16[32,192,128]{2,1,0:T(8,128)(2,1)} async-done(((f16[32,192,128]{2,1,0:T(8,128)(2,1)}), f16[32,192,128]{2,1,0:T(8,128)(2,1)}, u32[]{:S(2)}, u32[]{:S(2)}) %all-to-all-start.1) | async-done | bytes 1572896 | tf_op jit(solution)/shard_map/all_to_all | solution.py:218
  84.7 1.4 multiply_convert_fusion.v_ref
  86.2 6.2 %on_cells.2 = bf16[32,96,128]{2,1,0:T(8,128)(2,1)} custom-call(s32[3]{0:T(128)S(1)} %pad_add_fusion.where_ref, bf16[384,1536]{1,0:T(8,128)(2,1)} %constant_dynamic-update-slice_fusion.own_ref, bf16[384,1536]{1,0:T(8,128)(2,1)S(1)} %constant_dynamic-update-slice_fusion.4.own_far_ref, bf16[384,1536]{1,0:T(8,128)(2,1)} %collective-permute-done.7.other_ref, ...), custom_call_target="tpu_custom_call" | custom-call | tf_op jit(solution)/shard_map/on_cells/pallas_call | solution.py:186
  92.3 5.8 %all-to-all-start.2 = ((bf16[32,96,128]{2,1,0:T(8,128)(2,1)}), bf16[32,96,128]{2,1,0:T(8,128)(2,1)S(1)}, u32[]{:S(2)}, u32[]{:S(2)}) async-start(bf16[32,96,128]{2,1,0:T(8,128)(2,1)} %on_cells.2), calls=%async_computation.2 | async-start | bytes 1572864 | tf_op jit(solution)/shard_map/all_to_all | solution.py:218
  98.2 1.9 %multiply_add_fusion.3 = (f32[32,48,128]{2,1,0:T(8,128)S(1)}, f32[32,48,128]{2,1,0:T(8,128)S(1)}) fusion(f16[32,48,128]{2,1,0:T(8,128)(2,1)} %collective-permute-done.9, f32[32,96,128]{2,1,0:T(8,128)} %copy-done.2, f32[48]{0:T(128)S(1)} %get-tuple-element.67, f32[32,128]{1,0:T(8,128)S(1)} %multiply_bitcast_fusion, f32[48]{0:T(128)S(1)} %get-tuple-element.68, ...), kind=kLoop, calls=%fused_computation.8 | loop fusion | flops 1572864 | bytes 3948928 | tf_op jit(solution)/shard_map/add | solution.py:263
  100.1 1.3 fusion.2
  101.4 5.9 %collective-permute-start.12 = (f16[32,48,128]{2,1,0:T(8,128)(2,1)S(1)}, f16[32,48,128]{2,1,0:T(8,128)(2,1)S(1)}, u32[]{:S(2)}, u32[]{:S(2)}) collective-permute-start(f16[32,48,128]{2,1,0:T(8,128)(2,1)S(1)} %get-tuple-element.54), channel_id=1, source_target_pairs={{32,0},{64,32},{96,64},{128,96},{160,128},{192,160},{224,192},{33,... | collective-permute-start | bytes 1179656 | tf_op jit(solution)/shard_map/ppermute | solution.py:225
  107.3 1.9 %collective-permute-start.11 = (f16[32,48,128]{2,1,0:T(8,128)(2,1)S(1)}, f16[32,48,128]{2,1,0:T(8,128)(2,1)}, u32[]{:S(2)}, u32[]{:S(2)}) collective-permute-start(f16[32,48,128]{2,1,0:T(8,128)(2,1)S(1)} %get-tuple-element.55), channel_id=1, source_target_pairs={{0,32},{32,64},{64,96},{96,128},{128,160},{160,192},{192,224},{1,3... | collective-permute-start | bytes 1179656 | tf_op jit(solution)/shard_map/ppermute | solution.py:225
  109.2 1.3 pad_maximum_fusion.1.refs_0_
  110.5 1.8 %add_convert_fusion.v_ref = bf16[32,96,128]{2,1,0:T(8,128)(2,1)S(1)} fusion(bf16[32,96,128]{2,1,0:T(8,128)(2,1)} %on_cells.2, f16[32,192,128]{2,1,0:T(8,128)(2,1)} %all-to-all-done.1, f32[128]{0:T(128)S(1)} %dynamic-slice_multiply_fusion), kind=kLoop, calls=%fused_computation.2 | loop fusion | flops 2359296 | bytes 2359808 | tf_op jit(solution)/shard_map/convert_element_type | solution.py:277
  112.5 6.2 %on_cells.3 = bf16[32,96,128]{2,1,0:T(8,128)(2,1)} custom-call(s32[3]{0:T(128)S(1)} %pad_add_fusion.where_ref, bf16[384,1536]{1,0:T(8,128)(2,1)} %constant_dynamic-update-slice_fusion.own_ref, bf16[384,1536]{1,0:T(8,128)(2,1)S(1)} %copy-done.5, bf16[384,1536]{1,0:T(8,128)(2,1)} %collective-permute-done.7.other_ref, ...), custom_call_target="tpu_custom_call" | custom-call | tf_op jit(solution)/shard_map/on_cells/pallas_call | solution.py:186
  118.7 1.0 collective-permute-done.12
  119.6 6.3 %collective-permute-done.11 = f16[32,48,128]{2,1,0:T(8,128)(2,1)} collective-permute-done((f16[32,48,128]{2,1,0:T(8,128)(2,1)S(1)}, f16[32,48,128]{2,1,0:T(8,128)(2,1)}, u32[]{:S(2)}, u32[]{:S(2)}) %collective-permute-start.11) | collective-permute-done | bytes 393248 | tf_op jit(solution)/shard_map/ppermute | solution.py:225
  126.0 7.0 %all-to-all-start.3 = ((bf16[32,96,128]{2,1,0:T(8,128)(2,1)}), bf16[32,96,128]{2,1,0:T(8,128)(2,1)S(1)}, u32[]{:S(2)}, u32[]{:S(2)}) async-start(bf16[32,96,128]{2,1,0:T(8,128)(2,1)} %on_cells.3), calls=%async_computation.3 | async-start | bytes 1572864 | tf_op jit(solution)/shard_map/all_to_all | solution.py:218
  133.1 2.8 %collective-permute-start.14 = (bf16[32,48,128]{2,1,0:T(8,128)(2,1)S(1)}, bf16[32,48,128]{2,1,0:T(8,128)(2,1)S(1)}, u32[]{:S(2)}, u32[]{:S(2)}) collective-permute-start(bf16[32,48,128]{2,1,0:T(8,128)(2,1)S(1)} %get-tuple-element.58), channel_id=1, source_target_pairs={{32,0},{64,32},{96,64},{128,96},{160,128},{192,160},{224,192},{33,... | collective-permute-start | bytes 1179656 | tf_op jit(solution)/shard_map/ppermute | solution.py:225
  135.9 3.3 %collective-permute-start.13 = (bf16[32,48,128]{2,1,0:T(8,128)(2,1)S(1)}, bf16[32,48,128]{2,1,0:T(8,128)(2,1)S(1)}, u32[]{:S(2)}, u32[]{:S(2)}) collective-permute-start(bf16[32,48,128]{2,1,0:T(8,128)(2,1)S(1)} %get-tuple-element.59), channel_id=1, source_target_pairs={{0,32},{32,64},{64,96},{96,128},{128,160},{160,192},{192,224},{1,3... | collective-permute-start | bytes 1179656 | tf_op jit(solution)/shard_map/ppermute | solution.py:225
  139.2 9.2 %next_part.1 = (f32[2,48,4096]{2,1,0:T(8,128)}, f32[32,96,128]{2,1,0:T(8,128)S(1)}) custom-call(f32[2,48,4096]{2,1,0:T(8,128)S(1)} %copy-done.1, f32[48,8]{1,0:T(8,128)S(1)} %copy.18.coef_ref, f32[1,4096]{1,0:T(1,128)S(1)} %bitcast.35, f32[128,128]{1,0:T(8,128)S(1)} %copy-done.13, f32[32,32]{1,0:T(8,128)S(1)} %copy-done.14, f32[32,96,128]{2,1,0:T(8,128)S(1)} %copy-done.3, ...), custom_call_target="tpu_custom_call" | custom-call | tf_op jit(solution)/shard_map/next_part/pallas_call | solution.py:117
  148.4 1.1 copy-done.10
  149.6 4.7 %collective-permute-done.13 = bf16[32,48,128]{2,1,0:T(8,128)(2,1)S(1)} collective-permute-done((bf16[32,48,128]{2,1,0:T(8,128)(2,1)S(1)}, bf16[32,48,128]{2,1,0:T(8,128)(2,1)S(1)}, u32[]{:S(2)}, u32[]{:S(2)}) %collective-permute-start.13) | collective-permute-done | bytes 393248 | tf_op jit(solution)/shard_map/ppermute | solution.py:225
  154.3 2.2 %multiply_add_fusion = (f32[32,48,128]{2,1,0:T(8,128)S(1)}, f32[32,48,128]{2,1,0:T(8,128)}) fusion(bf16[32,48,128]{2,1,0:T(8,128)(2,1)S(1)} %collective-permute-done.14, f16[32,48,128]{2,1,0:T(8,128)(2,1)S(1)} %copy-done.16, f32[32,128]{1,0:T(8,128)S(1)} %multiply_bitcast_fusion, bf16[32,48,128]{2,1,0:T(8,128)(2,1)S(1)} %collective-permute-done.13, ...), kind=kLoop, calls=%fused_computation.5 | loop fusion | flops 1966080 | bytes 3162112 | tf_op jit(solution)/shard_map/add | solution.py:283
  156.4 1.1 copy-done.8
  157.6 1.5 add_last.1
  (79 shorter events, 4.0 us)
Async XLA Ops:
  0.6 0.9 copy-start
  2.3 34.3 %all-to-all-start = ((bf16[8,48,384]{2,1,0:T(8,128)(2,1)}), bf16[8,48,384]{2,1,0:T(8,128)(2,1)}, u32[]{:S(2)}, u32[]{:S(2)}) async-start(bf16[8,48,384]{2,1,0:T(8,128)(2,1)} %broadcast_in_dim.2), calls=%async_computation | async-start | bytes 589824 | tf_op jit(solution)/shard_map/all_to_all | solution.py:201
  12.3 11.8 %copy-start.20 = (s32[16]{0:T(128)S(1)}, s32[16]{0:T(128)}, u32[]{:S(2)}) copy-start(s32[16]{0:T(128)} %param.13) | copy-start | bytes 196
  12.3 11.9 %copy-start.18 = (s32[48]{0:T(128)S(1)}, s32[48]{0:T(128)}, u32[]{:S(2)}) copy-start(s32[48]{0:T(128)} %param.14) | copy-start | bytes 580
  12.3 11.9 %copy-start.19 = (f32[48]{0:T(128)S(1)}, f32[48]{0:T(128)}, u32[]{:S(2)}) copy-start(f32[48]{0:T(128)} %param.16) | copy-start | bytes 580
  12.4 12.1 %copy-start.17 = (f32[48]{0:T(128)S(1)}, f32[48]{0:T(128)}, u32[]{:S(2)}) copy-start(f32[48]{0:T(128)} %param.15) | copy-start | bytes 580
  12.4 12.3 %copy-start.1 = (f32[2,48,4096]{2,1,0:T(8,128)S(1)}, f32[2,48,4096]{2,1,0:T(8,128)}, u32[]{:S(2)}) copy-start(f32[2,48,4096]{2,1,0:T(8,128)} %prev_ref.3) | copy-start | bytes 4718596
  12.4 12.3 %copy-start.9 = (f32[2,48,4096]{2,1,0:T(8,128)S(1)}, f32[2,48,4096]{2,1,0:T(8,128)}, u32[]{:S(2)}) copy-start(f32[2,48,4096]{2,1,0:T(8,128)} %prev_ref.2) | copy-start | bytes 4718596
  12.4 12.3 %copy-start.12 = (f32[4096]{0:T(1024)S(1)}, f32[4096]{0:T(1024)}, u32[]{:S(2)}) copy-start(f32[4096]{0:T(1024)} %param.17) | copy-start | bytes 49156
  12.4 12.3 %copy-start.13 = (f32[128,128]{1,0:T(8,128)S(1)}, f32[128,128]{1,0:T(8,128)}, u32[]{:S(2)}) copy-start(f32[128,128]{1,0:T(8,128)} %long_ref.3) | copy-start | bytes 196612
  12.4 12.3 %copy-start.14 = (f32[32,32]{1,0:T(8,128)S(1)}, f32[32,32]{1,0:T(8,128)}, u32[]{:S(2)}) copy-start(f32[32,32]{1,0:T(8,128)} %short_ref.3) | copy-start | bytes 12292
  13.5 19.7 %collective-permute-start.9 = (f16[32,48,128]{2,1,0:T(8,128)(2,1)}, f16[32,48,128]{2,1,0:T(8,128)(2,1)}, u32[]{:S(2)}, u32[]{:S(2)}) collective-permute-start(f16[32,48,128]{2,1,0:T(8,128)(2,1)} %bitcast.31), channel_id=1, source_target_pairs={{0,32},{32,64},{64,96},{96,128},{128,160},{160,192},{192,224},{1,3... | collective-permute-start | bytes 1179656 | tf_op jit(solution)/shard_map/ppermute | solution.py:225
  18.0 15.1 %collective-permute-start.10 = (f16[32,48,128]{2,1,0:T(8,128)(2,1)}, f16[32,48,128]{2,1,0:T(8,128)(2,1)}, u32[]{:S(2)}, u32[]{:S(2)}) collective-permute-start(f16[32,48,128]{2,1,0:T(8,128)(2,1)} %bitcast.30), channel_id=1, source_target_pairs={{32,0},{64,32},{96,64},{128,96},{160,128},{192,160},{224,192},{33,... | collective-permute-start | bytes 1179656 | tf_op jit(solution)/shard_map/ppermute | solution.py:225
  32.8 2.1 %copy-start.2 = (f32[32,96,128]{2,1,0:T(8,128)}, f32[32,96,128]{2,1,0:T(8,128)S(1)}, u32[]{:S(2)}) copy-start(f32[32,96,128]{2,1,0:T(8,128)S(1)} %get-tuple-element.40) | copy-start | bytes 4718596
  36.6 48.1 %all-to-all-start.1 = ((f16[32,192,128]{2,1,0:T(8,128)(2,1)}), f16[32,192,128]{2,1,0:T(8,128)(2,1)}, u32[]{:S(2)}, u32[]{:S(2)}) async-start(f16[32,192,128]{2,1,0:T(8,128)(2,1)} %pad_maximum_fusion), calls=%async_computation.1 | async-start | bytes 3145728 | tf_op jit(solution)/shard_map/all_to_all | solution.py:218
  45.5 11.7 %collective-permute-start.3 = (bf16[384,384]{1,0:T(8,128)(2,1)}, bf16[384,384]{1,0:T(8,128)(2,1)S(1)}, u32[]{:S(2)}, u32[]{:S(2)}) collective-permute-start(bf16[384,384]{1,0:T(8,128)(2,1)} %bitcast.4), channel_id=1, source_target_pairs={{0,64},{32,96},{64,0},{96,32},{1,65},{33,97},{65,1},{97,33},{2,66}... | collective-permute-start | bytes 884744 | tf_op jit(solution)/shard_map/ppermute | solution.py:205
  45.6 14.4 %collective-permute-start.2 = (bf16[384,384]{1,0:T(8,128)(2,1)}, bf16[384,384]{1,0:T(8,128)(2,1)S(1)}, u32[]{:S(2)}, u32[]{:S(2)}) collective-permute-start(bf16[384,384]{1,0:T(8,128)(2,1)} %bitcast.4), channel_id=1, source_target_pairs={{0,96},{32,0},{64,32},{96,64},{1,97},{33,1},{65,33},{97,65},{2,98}... | collective-permute-start | bytes 884744 | tf_op jit(solution)/shard_map/ppermute | solution.py:205
  46.7 16.0 %collective-permute-start.1 = (bf16[384,384]{1,0:T(8,128)(2,1)}, bf16[384,384]{1,0:T(8,128)(2,1)S(1)}, u32[]{:S(2)}, u32[]{:S(2)}) collective-permute-start(bf16[384,384]{1,0:T(8,128)(2,1)} %bitcast.4), channel_id=1, source_target_pairs={{0,32},{32,64},{64,96},{96,0},{1,33},{33,65},{65,97},{97,1},{2,34}... | collective-permute-start | bytes 884744 | tf_op jit(solution)/shard_map/ppermute | solution.py:205
  47.7 15.7 %collective-permute-start = (bf16[384,384]{1,0:T(8,128)(2,1)}, bf16[384,384]{1,0:T(8,128)(2,1)S(1)}, u32[]{:S(2)}, u32[]{:S(2)}) collective-permute-start(bf16[384,384]{1,0:T(8,128)(2,1)} %bitcast.4), channel_id=1, source_target_pairs={{0,2},{2,0},{1,3},{3,1},{4,6},{6,4},{5,7},{7,5},{8,10},{10,8},{9,1... | collective-permute-start | bytes 884744 | tf_op jit(solution)/shard_map/ppermute | solution.py:209
  63.4 11.5 %collective-permute-start.6 = (bf16[384,384]{1,0:T(8,128)(2,1)S(1)}, bf16[384,384]{1,0:T(8,128)(2,1)S(1)}, u32[]{:S(2)}, u32[]{:S(2)}) collective-permute-start(bf16[384,384]{1,0:T(8,128)(2,1)S(1)} %collective-permute-done), channel_id=1, source_target_pairs={{0,64},{32,96},{64,0},{96,32},{1,65},{33,97},{65,1},{97,33},{2,66}... | collective-permute-start | bytes 884744 | tf_op jit(solution)/shard_map/ppermute | solution.py:205
  65.2 13.1 %collective-permute-start.5 = (bf16[384,384]{1,0:T(8,128)(2,1)S(1)}, bf16[384,384]{1,0:T(8,128)(2,1)S(1)}, u32[]{:S(2)}, u32[]{:S(2)}) collective-permute-start(bf16[384,384]{1,0:T(8,128)(2,1)S(1)} %collective-permute-done), channel_id=1, source_target_pairs={{0,96},{32,0},{64,32},{96,64},{1,97},{33,1},{65,33},{97,65},{2,98}... | collective-permute-start | bytes 884744 | tf_op jit(solution)/shard_map/ppermute | solution.py:205
  66.4 13.2 %collective-permute-start.4 = (bf16[384,384]{1,0:T(8,128)(2,1)S(1)}, bf16[384,384]{1,0:T(8,128)(2,1)S(1)}, u32[]{:S(2)}, u32[]{:S(2)}) collective-permute-start(bf16[384,384]{1,0:T(8,128)(2,1)S(1)} %collective-permute-done), channel_id=1, source_target_pairs={{0,32},{32,64},{64,96},{96,0},{1,33},{33,65},{65,97},{97,1},{2,34}... | collective-permute-start | bytes 884744 | tf_op jit(solution)/shard_map/ppermute | solution.py:205
  71.3 14.8 %collective-permute-start.7 = (bf16[384,1536]{1,0:T(8,128)(2,1)}, bf16[384,1536]{1,0:T(8,128)(2,1)}, u32[]{:S(2)}, u32[]{:S(2)}) collective-permute-start(bf16[384,1536]{1,0:T(8,128)(2,1)} %constant_dynamic-update-slice_fusion.own_ref), channel_id=1, source_target_pairs={{0,1},{1,0},{2,3},{3,2},{4,5},{5,4},{6,7},{7,6},{8,9},{9,8},{10,11... | collective-permute-start | bytes 3538952 | tf_op jit(solution)/shard_map/ppermute | solution.py:214
  79.7 12.6 %copy-start.4 = (bf16[384,1536]{1,0:T(8,128)(2,1)}, bf16[384,1536]{1,0:T(8,128)(2,1)S(1)}, u32[]{:S(2)}) copy-start(bf16[384,1536]{1,0:T(8,128)(2,1)S(1)} %constant_dynamic-update-slice_fusion.4.own_far_ref) | copy-start | bytes 3538948
  79.7 6.4 %collective-permute-start.8 = (bf16[384,1536]{1,0:T(8,128)(2,1)S(1)}, bf16[384,1536]{1,0:T(8,128)(2,1)}, u32[]{:S(2)}, u32[]{:S(2)}) collective-permute-start(bf16[384,1536]{1,0:T(8,128)(2,1)S(1)} %constant_dynamic-update-slice_fusion.4.own_far_ref), channel_id=1, source_target_pairs={{0,1},{1,0},{2,3},{3,2},{4,5},{5,4},{6,7},{7,6},{8,9},{9,8},{10,11... | collective-permute-start | bytes 3538952 | tf_op jit(solution)/shard_map/ppermute | solution.py:214
  84.7 1.4 copy-start.6
  92.3 33.6 %all-to-all-start.2 = ((bf16[32,96,128]{2,1,0:T(8,128)(2,1)}), bf16[32,96,128]{2,1,0:T(8,128)(2,1)S(1)}, u32[]{:S(2)}, u32[]{:S(2)}) async-start(bf16[32,96,128]{2,1,0:T(8,128)(2,1)} %on_cells.2), calls=%async_computation.2 | async-start | bytes 1572864 | tf_op jit(solution)/shard_map/all_to_all | solution.py:218
  101.4 18.2 %collective-permute-start.12 = (f16[32,48,128]{2,1,0:T(8,128)(2,1)S(1)}, f16[32,48,128]{2,1,0:T(8,128)(2,1)S(1)}, u32[]{:S(2)}, u32[]{:S(2)}) collective-permute-start(f16[32,48,128]{2,1,0:T(8,128)(2,1)S(1)} %get-tuple-element.54), channel_id=1, source_target_pairs={{32,0},{64,32},{96,64},{128,96},{160,128},{192,160},{224,192},{33,... | collective-permute-start | bytes 1179656 | tf_op jit(solution)/shard_map/ppermute | solution.py:225
  107.3 18.7 %collective-permute-start.11 = (f16[32,48,128]{2,1,0:T(8,128)(2,1)S(1)}, f16[32,48,128]{2,1,0:T(8,128)(2,1)}, u32[]{:S(2)}, u32[]{:S(2)}) collective-permute-start(f16[32,48,128]{2,1,0:T(8,128)(2,1)S(1)} %get-tuple-element.55), channel_id=1, source_target_pairs={{0,32},{32,64},{64,96},{96,128},{128,160},{160,192},{192,224},{1,3... | collective-permute-start | bytes 1179656 | tf_op jit(solution)/shard_map/ppermute | solution.py:225
  110.5 1.8 %copy-start.5 = (bf16[384,1536]{1,0:T(8,128)(2,1)S(1)}, bf16[384,1536]{1,0:T(8,128)(2,1)}, u32[]{:S(2)}) copy-start(bf16[384,1536]{1,0:T(8,128)(2,1)} %copy-done.4) | copy-start | bytes 3538948
  110.5 2.0 %copy-start.7 = (f32[1536,128]{1,0:T(8,128)S(1)}, f32[1536,128]{1,0:T(8,128)}, u32[]{:S(2)}) copy-start(f32[1536,128]{1,0:T(8,128)} %param.18) | copy-start | bytes 2359300
  119.6 6.4 %copy-start.15 = (f16[32,48,128]{2,1,0:T(8,128)(2,1)}, f16[32,48,128]{2,1,0:T(8,128)(2,1)S(1)}, u32[]{:S(2)}) copy-start(f16[32,48,128]{2,1,0:T(8,128)(2,1)S(1)} %collective-permute-done.12) | copy-start | bytes 1179652
  126.0 30.5 %all-to-all-start.3 = ((bf16[32,96,128]{2,1,0:T(8,128)(2,1)}), bf16[32,96,128]{2,1,0:T(8,128)(2,1)S(1)}, u32[]{:S(2)}, u32[]{:S(2)}) async-start(bf16[32,96,128]{2,1,0:T(8,128)(2,1)} %on_cells.3), calls=%async_computation.3 | async-start | bytes 1572864 | tf_op jit(solution)/shard_map/all_to_all | solution.py:218
  133.0 6.2 %copy-start.3 = (f32[32,96,128]{2,1,0:T(8,128)S(1)}, f32[32,96,128]{2,1,0:T(8,128)}, u32[]{:S(2)}) copy-start(f32[32,96,128]{2,1,0:T(8,128)} %pad_maximum_fusion.1.refs_0_) | copy-start | bytes 4718596
  133.1 16.5 %collective-permute-start.14 = (bf16[32,48,128]{2,1,0:T(8,128)(2,1)S(1)}, bf16[32,48,128]{2,1,0:T(8,128)(2,1)S(1)}, u32[]{:S(2)}, u32[]{:S(2)}) collective-permute-start(bf16[32,48,128]{2,1,0:T(8,128)(2,1)S(1)} %get-tuple-element.58), channel_id=1, source_target_pairs={{32,0},{64,32},{96,64},{128,96},{160,128},{192,160},{224,192},{33,... | collective-permute-start | bytes 1179656 | tf_op jit(solution)/shard_map/ppermute | solution.py:225
  135.9 18.4 %copy-start.16 = (f16[32,48,128]{2,1,0:T(8,128)(2,1)S(1)}, f16[32,48,128]{2,1,0:T(8,128)(2,1)}, u32[]{:S(2)}) copy-start(f16[32,48,128]{2,1,0:T(8,128)(2,1)} %copy-done.15) | copy-start | bytes 1179652
  135.9 18.4 %collective-permute-start.13 = (bf16[32,48,128]{2,1,0:T(8,128)(2,1)S(1)}, bf16[32,48,128]{2,1,0:T(8,128)(2,1)S(1)}, u32[]{:S(2)}, u32[]{:S(2)}) collective-permute-start(bf16[32,48,128]{2,1,0:T(8,128)(2,1)S(1)} %get-tuple-element.59), channel_id=1, source_target_pairs={{0,32},{32,64},{64,96},{96,128},{128,160},{160,192},{192,224},{1,3... | collective-permute-start | bytes 1179656 | tf_op jit(solution)/shard_map/ppermute | solution.py:225
  148.4 1.1 copy-start.10
  149.6 6.9 %copy-start.11 = (f32[32,96,128]{2,1,0:T(8,128)S(1)}, f32[32,96,128]{2,1,0:T(8,128)}, u32[]{:S(2)}) copy-start(f32[32,96,128]{2,1,0:T(8,128)} %copy-done.10) | copy-start | bytes 4718596
  156.4 1.1 copy-start.8
